TPU v7x, 32 devices: a whole 2x2x4 slice. The times are simulated.
32 devices in a mesh: clips: 16 (over z, x, core), mlp: 2 (over y).
Axes of the slice: x: 2, y: 2, z: 4, core: 2. Of those that a mesh axis runs over, the one named last changes fastest.
Arguments:
- flat_params: bfloat16 [3804160], replicated
- w_fc1: bfloat16 [768, 3072], P(None, 'mlp'), may hold values from -0.21875 to 0.21875
- w_fc2: bfloat16 [3072, 768], P('mlp'), may hold values from -0.15625 to 0.15625
- w_up: bfloat16 [512, 2048], P(None, 'mlp'), may hold values from -0.25 to 0.25
- w_down: bfloat16 [2048, 512], P('mlp'), may hold values from -0.21875 to 0.21875
- patches: bfloat16 [9984, 768], P(('clips', 'mlp')), may hold values from -6 to 6
- clip_ids: int32 [49152], P(('clips', 'mlp')), may hold values from 0 to 2, as said below
- visible_index: int32 [9984], P(('clips', 'mlp')), may hold values from 0 to 1535, as said below
- cotangent: bfloat16 [49152, 512], P(('clips', 'mlp')), may hold values from -6 to 6
Outputs:
- decoded: bfloat16 [49152, 512], P(('clips', 'mlp'))
- input_grad: float32 [9984, 768], P(('clips', 'mlp'))
- param_grad: float32 [3804160], P('mlp')
- fc1_grad: float32 [768, 3072], P(None, 'mlp')
- fc2_grad: float32 [3072, 768], P('mlp')
- up_grad: float32 [512, 2048], P(None, 'mlp')
- down_grad: float32 [2048, 512], P('mlp')
Inputs may be any that keep to these rules, and one draw needn't show every extreme that they name: `clip_ids`: each buffer of 1536 patches is either one clip of 192 x 8 patches, all with id 0, or three clips of 512 patches with ids 0, 1, 2 in order; a clip's patch (t, f) is row t * 8 + f of it. Both kinds occur in every draw. `visible_index`: the 312 entries of a buffer are distinct and increasing positions within that buffer; a three-clip buffer has 104 of them in each clip.
All inputs are finite; a program needn't handle non-finite values.
Results may differ from a plain program's by a relative error of at most 0.028.
Values may be sent and summed in bfloat16 or wider, within the bound.
No kernel may reach another device: no remote copies, remote signals or barrier semaphores. Data moves between devices by JAX's collectives and lax.ppermute only.
A program may use at most 384 MiB of HBM per device.

v0:
```python
import math

import jax
import jax.numpy as jnp
from jax import lax
from jax.sharding import PartitionSpec as P

D = 768
HEADS = 12
DD = 512
DHEADS = 16
FREQ = 8
WIN = 4
LONG_FRAMES = 192
ROWS = 1536
VIS = 312
PARAMS = 3804160


EPSILON = 1e-06


def layer_norm(inputs, weight_gain):
    row_mean = jnp.mean(inputs, axis=-1, keepdims=True)
    centred = inputs - row_mean
    variance = jnp.mean(centred * centred, axis=-1, keepdims=True)
    return centred * lax.rsqrt(variance + EPSILON) * weight_gain


def exact_gelu(inputs):
    return jax.nn.gelu(inputs, approximate=False)


def unpack(flat):
    layout = ((D, 3 * D), (D, D), (D,), (D,), (D, DD), (DD,), (DD, 3 * DD), (DD, DD), (DD,), (DD,))
    members = []
    offset = 0
    for dims_of in layout:
        length = math.prod(dims_of)
        members.append(flat[offset : offset + length].reshape(dims_of))
        offset = offset + length
    return members


def to_windows(source, head_count):
    head_size = source.shape[-1] // head_count
    blocks = source.reshape(-1, LONG_FRAMES // WIN, WIN, FREQ // WIN, WIN, head_count, head_size)
    blocks = blocks.transpose(0, 1, 3, 2, 4, 5, 6)
    return blocks.reshape(-1, WIN * WIN, head_count, head_size)


def from_windows(source, buffers):
    blocks = source.reshape(buffers, LONG_FRAMES // WIN, FREQ // WIN, WIN, WIN, -1)
    blocks = blocks.transpose(0, 1, 3, 2, 4, 5)
    return blocks.reshape(buffers * ROWS, -1)


def matmul(left, right):
    return jnp.dot(left, right, preferred_element_type=jnp.float32)


def transposed(left, right):
    return lax.dot_general(
        left, right, (((0,), (0,)), ((), ())), preferred_element_type=jnp.float32
    )


def against(left, right):
    return lax.dot_general(
        left, right, (((1,), (1,)), ((), ())), preferred_element_type=jnp.float32
    )


def score_table(queries, key_rows, allowed):
    factor = 1.0 / math.sqrt(queries.shape[-1])
    scores = (
        jnp.einsum("bqhd,bkhd->bhqk", queries, key_rows, preferred_element_type=jnp.float32)
        * factor
    )
    if allowed is not None:
        scores = jnp.where(allowed, scores, -1e30)
    return scores


def attend_forward(queries, key_rows, val_rows, allowed):
    scores = score_table(queries, key_rows, allowed)
    highest = jnp.max(scores, axis=-1, keepdims=True)
    expont = jnp.exp(scores - highest)
    total_row = jnp.sum(expont, axis=-1, keepdims=True)
    attn_probs = (expont / total_row).astype(jnp.bfloat16)
    mixed = jnp.einsum("bhqk,bkhd->bqhd", attn_probs, val_rows, preferred_element_type=jnp.float32)
    return (mixed, highest + jnp.log(total_row))


def attend_backward(queries, key_rows, val_rows, allowed, log_total, mix_grad):
    factor = 1.0 / math.sqrt(queries.shape[-1])
    attn_probs = jnp.exp(score_table(queries, key_rows, allowed) - log_total)
    prob_grad = jnp.einsum(
        "bqhd,bkhd->bhqk", mix_grad, val_rows, preferred_element_type=jnp.float32
    )
    score_grad = (
        attn_probs * (prob_grad - jnp.sum(attn_probs * prob_grad, axis=-1, keepdims=True))
    ).astype(jnp.bfloat16)
    query_grad = (
        jnp.einsum("bhqk,bkhd->bqhd", score_grad, key_rows, preferred_element_type=jnp.float32)
        * factor
    )
    key_grad = (
        jnp.einsum("bhqk,bqhd->bkhd", score_grad, queries, preferred_element_type=jnp.float32)
        * factor
    )
    value_grad = jnp.einsum(
        "bhqk,bqhd->bkhd",
        attn_probs.astype(jnp.bfloat16),
        mix_grad,
        preferred_element_type=jnp.float32,
    )
    return (query_grad, key_grad, value_grad)


def shards(flat_params, w_fc1, w_fc2, w_up, w_down, patches, clip_ids, visible_index, cotangent):
    w_qkv, w_proj, g_one, g_two, w_embed, mask_token, w_dqkv, w_dproj, gd_one, gd_two = unpack(
        flat_params
    )
    buffers = patches.shape[0] // VIS
    rows_here = cotangent.shape[0]
    head_size = D // HEADS
    visible = visible_index.reshape(buffers, VIS)
    segment = jnp.take_along_axis(clip_ids.reshape(buffers, ROWS), visible, axis=1)
    allowed = (segment[:, :, None] == segment[:, None, :])[:, None]
    inputs = patches.astype(jnp.float32)
    enc_norm, norm_pull1 = jax.vjp(layer_norm, inputs, g_one.astype(jnp.float32))
    enc_norm = enc_norm.astype(jnp.bfloat16)
    enc_qkv = (
        matmul(enc_norm, w_qkv).astype(jnp.bfloat16).reshape(buffers, VIS, 3, HEADS, head_size)
    )
    enc_query, enc_key, enc_value = (enc_qkv[:, :, 0], enc_qkv[:, :, 1], enc_qkv[:, :, 2])
    enc_out, enc_lse = attend_forward(enc_query, enc_key, enc_value, allowed)
    enc_mix = enc_out.reshape(-1, D).astype(jnp.bfloat16)
    first = inputs + matmul(enc_mix, w_proj)
    enc_in2, norm_pull2 = jax.vjp(layer_norm, first, g_two.astype(jnp.float32))
    enc_in2 = enc_in2.astype(jnp.bfloat16)
    enc_all = lax.all_gather(enc_in2, "mlp", axis=0, tiled=True)
    enc_act, gelu_pull1 = jax.vjp(exact_gelu, matmul(enc_all, w_fc1))
    enc_hidden = enc_act.astype(jnp.bfloat16)
    second = first + lax.psum_scatter(
        matmul(enc_hidden, w_fc2), "mlp", scatter_dimension=0, tiled=True
    )
    second_low = second.astype(jnp.bfloat16)
    embedded = matmul(second_low, w_embed).astype(jnp.bfloat16)
    matches = visible[:, None, :] == jnp.arange(ROWS, dtype=jnp.int32)[None, :, None]
    filled = jnp.einsum(
        "brv,bvd->brd",
        matches.astype(jnp.bfloat16),
        embedded.reshape(buffers, VIS, DD),
        preferred_element_type=jnp.float32,
    )
    masked_rows = 1.0 - jnp.any(matches, axis=2).astype(jnp.float32)
    start = (filled + masked_rows[:, :, None] * mask_token.astype(jnp.float32)).reshape(
        rows_here, DD
    )
    dec_norm, norm_pull3 = jax.vjp(layer_norm, start, gd_one.astype(jnp.float32))
    dec_norm = dec_norm.astype(jnp.bfloat16)
    dec_qkv = matmul(dec_norm, w_dqkv).astype(jnp.bfloat16)
    dec_query = to_windows(dec_qkv[:, :DD], DHEADS)
    dec_key = to_windows(dec_qkv[:, DD : 2 * DD], DHEADS)
    dec_value = to_windows(dec_qkv[:, 2 * DD :], DHEADS)
    dec_out, dec_lse = attend_forward(dec_query, dec_key, dec_value, None)
    dec_mix = from_windows(dec_out, buffers).astype(jnp.bfloat16)
    middle = start + matmul(dec_mix, w_dproj)
    dec_in2, norm_pull4 = jax.vjp(layer_norm, middle, gd_two.astype(jnp.float32))
    dec_in2 = dec_in2.astype(jnp.bfloat16)
    rows_all = lax.all_gather(dec_in2, "mlp", axis=0, tiled=True)
    dec_act, gelu_pull2 = jax.vjp(exact_gelu, matmul(rows_all, w_up))
    dec_hidden = dec_act.astype(jnp.bfloat16)
    decoded_full = middle + lax.psum_scatter(
        matmul(dec_hidden, w_down).astype(jnp.bfloat16), "mlp", scatter_dimension=0, tiled=True
    ).astype(jnp.float32)
    upstream_all = lax.all_gather(cotangent, "mlp", axis=0, tiled=True)
    down_grad_part = transposed(dec_hidden, upstream_all)
    pre_grad = gelu_pull2(against(upstream_all, w_down))[0].astype(jnp.bfloat16)
    up_grad_part = transposed(rows_all, pre_grad)
    in2_grad = lax.psum_scatter(
        against(pre_grad, w_up).astype(jnp.bfloat16), "mlp", scatter_dimension=0, tiled=True
    ).astype(jnp.float32)
    decoded = decoded_full.astype(jnp.bfloat16)
    middle_part, gd_two_grad = norm_pull4(in2_grad)
    middle_grad = cotangent.astype(jnp.float32) + middle_part
    dec_branch = middle_grad.astype(jnp.bfloat16)
    dproj_grad = transposed(dec_mix, dec_branch)
    dec_mix_grad = to_windows(against(dec_branch, w_dproj).astype(jnp.bfloat16), DHEADS)
    dq_grad, dk_grad, dv_grad = attend_backward(
        dec_query, dec_key, dec_value, None, dec_lse, dec_mix_grad
    )
    dec_qkv_grad = jnp.concatenate(
        [
            from_windows(dq_grad, buffers),
            from_windows(dk_grad, buffers),
            from_windows(dv_grad, buffers),
        ],
        axis=1,
    ).astype(jnp.bfloat16)
    dqkv_weight_grad = transposed(dec_norm, dec_qkv_grad)
    start_part, gd_one_grad = norm_pull3(against(dec_qkv_grad, w_dqkv))
    start_grad = (middle_grad + start_part).reshape(buffers, ROWS, DD)
    mask_grad = jnp.sum(start_grad * masked_rows[:, :, None], axis=(0, 1))
    embed_grad = (
        jnp.take_along_axis(start_grad, visible[:, :, None], axis=1)
        .reshape(-1, DD)
        .astype(jnp.bfloat16)
    )
    w_embed_grad = transposed(second_low, embed_grad)
    second_grad = against(embed_grad, w_embed)
    out_grad = second_grad.astype(jnp.bfloat16)
    out_all = lax.all_gather(out_grad, "mlp", axis=0, tiled=True)
    fc2_grad_part = transposed(enc_hidden, out_all)
    fc_pre_grad = gelu_pull1(against(out_all, w_fc2))[0].astype(jnp.bfloat16)
    fc1_grad_part = transposed(enc_all, fc_pre_grad)
    enc_in2_grad = lax.psum_scatter(
        against(fc_pre_grad, w_fc1).astype(jnp.bfloat16), "mlp", scatter_dimension=0, tiled=True
    ).astype(jnp.float32)
    first_part, g_two_grad = norm_pull2(enc_in2_grad)
    first_grad = second_grad + first_part
    enc_branch = first_grad.astype(jnp.bfloat16)
    proj_grad = transposed(enc_mix, enc_branch)
    enc_mix_grad = (
        against(enc_branch, w_proj).astype(jnp.bfloat16).reshape(buffers, VIS, HEADS, head_size)
    )
    eq_grad, ek_grad, ev_grad = attend_backward(
        enc_query, enc_key, enc_value, allowed, enc_lse, enc_mix_grad
    )
    enc_qkv_grad = (
        jnp.stack([eq_grad, ek_grad, ev_grad], axis=2).reshape(-1, 3 * D).astype(jnp.bfloat16)
    )
    qkv_weight_grad = transposed(enc_norm, enc_qkv_grad)
    input_part, g_one_grad = norm_pull1(against(enc_qkv_grad, w_qkv))
    input_grad = first_grad + input_part
    members = [
        qkv_weight_grad,
        proj_grad,
        g_one_grad,
        g_two_grad,
        w_embed_grad,
        mask_grad,
        dqkv_weight_grad,
        dproj_grad,
        gd_one_grad,
        gd_two_grad,
    ]
    flat_grad = jnp.concatenate(
        [member.reshape(-1) for member in members]
        + [jnp.zeros((flat_params.shape[0] - PARAMS,), jnp.float32)]
    )
    shard_grad = lax.psum_scatter(
        flat_grad.astype(jnp.bfloat16), "mlp", scatter_dimension=0, tiled=True
    )
    param_grad, fc1_grad, fc2_grad, up_grad, down_grad = (
        lax.psum(shard_grad, "clips").astype(jnp.float32),
        lax.psum(fc1_grad_part.astype(jnp.bfloat16), "clips").astype(jnp.float32),
        lax.psum(fc2_grad_part.astype(jnp.bfloat16), "clips").astype(jnp.float32),
        lax.psum(up_grad_part.astype(jnp.bfloat16), "clips").astype(jnp.float32),
        lax.psum(down_grad_part.astype(jnp.bfloat16), "clips").astype(jnp.float32),
    )
    return (decoded, input_grad, param_grad, fc1_grad, fc2_grad, up_grad, down_grad)


def solution(mesh):
    placed = (
        P(),
        P(None, "mlp"),
        P("mlp", None),
        P(None, "mlp"),
        P("mlp", None),
        P(("clips", "mlp"), None),
        P(("clips", "mlp")),
        P(("clips", "mlp")),
        P(("clips", "mlp"), None),
    )
    return jax.shard_map(
        shards,
        mesh=mesh,
        in_specs=placed,
        out_specs=(
            P(("clips", "mlp"), None),
            P(("clips", "mlp"), None),
            P("mlp"),
            P(None, "mlp"),
            P("mlp", None),
            P(None, "mlp"),
            P("mlp", None),
        ),
        check_vma=False,
    )
```

profile of v0, /device:TPU:0, one launch (start us, length us, event | category | flops | bytes accessed | tf_op | source)
XLA Modules:
  0.0 1081.1 jit_solution(7096899038210828048)
XLA Ops:
  44.2 14.8 %all_gather.12 = bf16[624,768]{1,0:T(8,128)(2,1)S(1)} all-gather(bf16[312,768]{1,0:T(8,128)(2,1)S(1)} %multiply_convert_fusion.8), channel_id=1, replica_groups=mesh['clips'=16,'mlp'=2] {'mlp'}, dimensions={0}, use_global_device_ids=true | all-gather | bytes 1437696 | tf_op jit(solution)/shard_map/all_gather | solution.py:143
  59.0 11.4 %multiply_convert_fusion.5 = (bf16[624,1536]{1,0:T(8,128)(2,1)S(1)}, f32[624,1536]{1,0:T(8,128)}, f32[624,1536]{1,0:T(8,128)}) fusion(bf16[624,768]{1,0:T(8,128)(2,1)S(1)} %all_gather.12, bf16[768,1536]{1,0:T(8,128)(2,1)S(1)} %copy-done), kind=kOutput, calls=%fused_computation.60 | convolution fusion | flops 1534500864 | bytes 12902400 | tf_op jit(solution)/shard_map/dot_general | solution.py:59
  91.4 14.7 %reduce-scatter.5.cloned.1.call-done = f32[312,768]{1,0:T(8,128)} async-done(((f32[624,768]{1,0:T(8,128)}), f32[312,768]{1,0:T(8,128)}) %reduce-scatter.5.cloned.1.call-update) | async-done | bytes 958480 | tf_op jit(solution)/shard_map/reduce_scatter | solution.py:146
  122.8 8.0 reshape.597
  130.8 9.1 copy.125
  139.8 8.3 reshape.599
  148.2 9.1 copy.126
  165.2 9.1 copy.124
  174.2 12.6 %multiply_reduce_fusion.1 = (f32[96,16,16]{2,1,0:T(8,128)S(1)}, f32[96,16,16,16]{2,3,1,0:T(8,128)}) fusion(bf16[96,16,16,32]{3,1,2,0:T(8,128)(2,1)} %bitcast.143, bf16[96,16,16,32]{3,1,2,0:T(8,128)(2,1)} %bitcast.139), kind=kOutput, calls=%fused_computation.27 | convolution fusion | flops 25927680 | bytes 4816896 | tf_op jit(solution)/shard_map/bqhd,bkhd->bhqk/dot_general | solution.py:77
  194.3 10.2 convert_bitcast_fusion.1
  204.6 8.0 copy.128
  212.6 9.1 convert_element_type.229
  236.1 44.3 %all-gather.3.cloned.1.call-done = bf16[3072,512]{0,1:T(8,128)(2,1)} async-done(((bf16[1536,512]{0,1:T(8,128)(2,1)}), bf16[3072,512]{0,1:T(8,128)(2,1)}) %all-gather.3.cloned.1.call-update) | async-done | bytes 3145744 | tf_op jit(solution)/shard_map/all_gather | solution.py:173
  280.4 33.6 %multiply_convert_fusion.3 = (bf16[3072,1024]{1,0:T(8,128)(2,1)}, f32[3072,1024]{1,0:T(8,128)}, f32[3072,1024]{1,0:T(8,128)}) fusion(bf16[3072,512]{0,1:T(8,128)(2,1)} %all-gather.3.cloned.1.call-done, bf16[512,1024]{1,0:T(8,128)(2,1)} %param.12), kind=kOutput, calls=%fused_computation.10 | convolution fusion | flops 3425697792 | bytes 35651584 | tf_op jit(solution)/shard_map/dot_general | solution.py:59
  314.0 12.9 %all-gather.5.cloned.1.call-done = bf16[3072,512]{1,0:T(8,128)(2,1)} async-done(((bf16[1536,512]{1,0:T(8,128)(2,1)}), bf16[3072,512]{1,0:T(8,128)(2,1)}) %all-gather.5.cloned.1.call-update) | async-done | bytes 3145744 | tf_op jit(solution)/shard_map/all_gather | solution.py:179
  326.9 14.1 %add_convert_fusion = bf16[3072,1024]{1,0:T(8,128)(2,1)S(1)} fusion(f32[3072,1024]{1,0:T(8,128)} %get-tuple-element.58, f32[3072,1024]{1,0:T(8,128)} %get-tuple-element.83, bf16[3072,512]{1,0:T(8,128)(2,1)} %all-gather.5.cloned.1.call-done, bf16[1024,512]{1,0:T(8,128)(2,1)} %param.13), kind=kOutput, calls=%fused_computation.9 | convolution fusion | flops 3265265664 | bytes 35651584 | tf_op jit(solution)/shard_map/dot_general | solution.py:69
  353.1 9.2 convolution_convert_fusion.3
  362.3 29.7 %reduce-scatter.9.cloned.1.call-done = bf16[1536,512]{0,1:T(8,128)(2,1)} async-done(((bf16[3072,512]{0,1:T(8,128)(2,1)}), bf16[1536,512]{0,1:T(8,128)(2,1)}) %reduce-scatter.9.cloned.1.call-update) | async-done | bytes 1572880 | tf_op jit(solution)/shard_map/reduce_scatter | solution.py:183
  402.0 8.1 reshape.601
  415.2 10.5 convert_bitcast_fusion
  425.7 8.0 copy.141
  433.7 9.1 reshape.607
  449.7 14.4 %multiply_reduce_fusion = (f32[96,16,16]{2,1,0:T(8,128)}, f32[96,16,16,16]{2,3,1,0:T(8,128)}) fusion(f32[96,16,16,16]{2,3,1,0:T(8,128)} %get-tuple-element.80, f32[96,16,16]{2,1,0:T(8,128)S(1)} %log_add_fusion, bf16[96,16,16,32]{3,1,2,0:T(8,128)(2,1)} %bitcast.146, bf16[96,16,16,32]{3,2,1,0:T(8,128)(2,1)} %bitcast.142), kind=kOutput, calls=%fused_computation.7 | convolution fusion | flops 26714112 | bytes 6488064 | tf_op jit(solution)/shard_map/bqhd,bkhd->bhqk/dot_general | solution.py:98
  464.2 10.3 multiply_convert_fusion.2
  474.5 8.5 fusion.11
  488.3 9.1 reshape.605
  515.6 9.1 reshape.603
  555.8 13.4 %all_gather.15 = bf16[624,768]{1,0:T(8,128)(2,1)S(1)} all-gather(bf16[312,768]{1,0:T(8,128)(2,1)S(1)} %get-tuple-element.88), channel_id=1, replica_groups=mesh['clips'=16,'mlp'=2] {'mlp'}, dimensions={0}, use_global_device_ids=true | all-gather | bytes 1437696 | tf_op jit(solution)/shard_map/all_gather | solution.py:215
  645.3 13.4 %dynamic-update-slice.4 = bf16[3804160]{0:T(1024)(128)(2,1)} dynamic-update-slice(bf16[3804160]{0:T(1024)(128)(2,1)} %dynamic-update-slice.3, bf16[393216]{0:T(1024)(128)(2,1)} %bitcast.162, s32[]{} %constant.44) | dynamic-update-slice | bytes 1572868
  668.7 8.3 convolution_convert_fusion.11
  691.4 157.8 %all-reduce.5.cloned.1.call-done = bf16[3804160]{0:T(1024)(128)(2,1)} async-done(((bf16[3804160]{0:T(1024)(128)(2,1)}), bf16[3804160]{0:T(1024)(128)(2,1)}) %all-reduce.5.cloned.1.call-update) | async-done | bytes 7608336
  859.3 201.2 %all-reduce.7.cloned.1.call-done = (bf16[1902080]{0:T(1024)(128)(2,1)}, bf16[768,1536]{1,0:T(8,128)(2,1)}, bf16[1536,768]{1,0:T(8,128)(2,1)}, bf16[512,1024]{1,0:T(8,128)(2,1)}, bf16[1024,512]{1,0:T(8,128)(2,1)}) async-done(((bf16[1902080]{0:T(1024)(128)(2,1)}, bf16[768,1536]{1,0:T(8,128)(2,1)}, bf16[1536,768]{1,0:T(8,128)(2,1)}, bf16[512,1024]{1,0:T(8,128)(2,1)}, bf16[1024,512]{1,0:T(8,128)(2,1)}), ...) | async-done | bytes 10619920 | tf_op jit(solution)/shard_map/psum | solution.py:258
  (327 shorter events, 316.0 us)
Async XLA Ops:
  7.2 51.8 %copy-start = (bf16[768,1536]{1,0:T(8,128)(2,1)S(1)}, bf16[768,1536]{1,0:T(8,128)(2,1)}, u32[]{:S(2)}) copy-start(bf16[768,1536]{1,0:T(8,128)(2,1)} %param.10) | copy-start | bytes 7077892
  7.2 98.9 %reduce-scatter.5.cloned.1.call-start = ((), (), s32[]{:S(2)}) async-start(), calls=%async_computation.4 | async-start | bytes 2875392 | tf_op jit(solution)/shard_map/reduce_scatter | solution.py:146
  8.1 11.5 %copy-start.56 = (f32[768]{0:T(1024)}, f32[768]{0:T(1024)S(1)}, u32[]{:S(2)}) copy-start(f32[768]{0:T(1024)S(1)} %get-tuple-element.67) | copy-start | bytes 9220
  8.1 35.9 %copy-start.46 = (f32[768]{0:T(1024)}, f32[768]{0:T(1024)S(1)}, u32[]{:S(2)}) copy-start(f32[768]{0:T(1024)S(1)} %get-tuple-element.66) | copy-start | bytes 9220
  11.7 12.4 %copy-start.58 = (f32[312]{0:T(512)}, f32[312]{0:T(512)S(1)}, u32[]{:S(2)}) copy-start(f32[312]{0:T(512)S(1)} %broadcast_multiply_fusion.3) | copy-start | bytes 3748
  12.0 12.1 %copy-start.68 = (f32[312]{0:T(512)}, f32[312]{0:T(512)S(1)}, u32[]{:S(2)}) copy-start(f32[312]{0:T(512)S(1)} %fusion.61) | copy-start | bytes 3748
  12.0 12.1 %copy-start.66 = (f32[312]{0:T(512)}, f32[312]{0:T(512)S(1)}, u32[]{:S(2)}) copy-start(f32[312]{0:T(512)S(1)} %fusion.68) | copy-start | bytes 3748
  19.6 8.2 copy-start.72
  43.7 62.4 %copy-start.8 = (f32[312,768]{1,0:T(8,128)}, f32[312,768]{1,0:T(8,128)S(1)}, u32[]{:S(2)}) copy-start(f32[312,768]{1,0:T(8,128)S(1)} %get-tuple-element.75) | copy-start | bytes 2875396
  43.7 26.7 %copy-start.50 = (f32[312]{0:T(512)}, f32[312]{0:T(512)S(1)}, u32[]{:S(2)}) copy-start(f32[312]{0:T(512)S(1)} %broadcast_multiply_fusion.2) | copy-start | bytes 3748
  43.9 26.5 %copy-start.70 = (f32[312]{0:T(512)}, f32[312]{0:T(512)S(1)}, u32[]{:S(2)}) copy-start(f32[312]{0:T(512)S(1)} %multiply_reduce_fusion.8) | copy-start | bytes 3748
  44.0 26.4 %copy-start.60 = (f32[312]{0:T(512)}, f32[312]{0:T(512)S(1)}, u32[]{:S(2)}) copy-start(f32[312]{0:T(512)S(1)} %fusion.69) | copy-start | bytes 3748
  59.0 11.4 %copy-start.36 = (bf16[624,768]{1,0:T(8,128)(2,1)}, bf16[624,768]{1,0:T(8,128)(2,1)S(1)}, u32[]{:S(2)}) copy-start(bf16[624,768]{1,0:T(8,128)(2,1)S(1)} %all_gather.12) | copy-start | bytes 2875396
  59.0 12.7 %copy-start.77 = (bf16[1536,768]{1,0:T(8,128)(2,1)S(1)}, bf16[1536,768]{1,0:T(8,128)(2,1)}, u32[]{:S(2)}) copy-start(bf16[1536,768]{1,0:T(8,128)(2,1)} %param.11) | copy-start | bytes 7077892
  74.6 205.8 %all-gather.3.cloned.1.call-start = ((), (), s32[]{:S(2)}) async-start(), calls=%async_computation.5 | async-start | bytes 4718592 | tf_op jit(solution)/shard_map/all_gather | solution.py:173
  91.3 24.0 %copy-start.64 = (f32[512]{0:T(512)}, f32[512]{0:T(512)S(1)}, u32[]{:S(2)}) copy-start(f32[512]{0:T(512)S(1)} %get-tuple-element.64) | copy-start | bytes 6148
  91.4 21.2 %copy-start.62 = (f32[1536]{0:T(1024)}, f32[1536]{0:T(1024)S(1)}, u32[]{:S(2)}) copy-start(f32[1536]{0:T(1024)S(1)} %convert_subtract_fusion.1) | copy-start | bytes 18436
  112.5 8.0 copy-start.44
  194.3 10.3 copy-start.25
  235.3 91.6 %all-gather.5.cloned.1.call-start = ((), (), s32[]{:S(2)}) async-start(), calls=%async_computation.7 | async-start | bytes 4718592 | tf_op jit(solution)/shard_map/all_gather | solution.py:179
  236.1 156.0 %reduce-scatter.9.cloned.1.call-start = ((), (), s32[]{:S(2)}) async-start(), calls=%async_computation.8 | async-start | bytes 4718592 | tf_op jit(solution)/shard_map/reduce_scatter | solution.py:183
  326.9 16.8 %copy-start.79 = (bf16[512,1024]{1,0:T(8,128)(2,1)S(1)}, bf16[512,1024]{1,0:T(8,128)(2,1)}, u32[]{:S(2)}) copy-start(bf16[512,1024]{1,0:T(8,128)(2,1)} %param.12) | copy-start | bytes 3145732
  348.5 191.8 %reduce-scatter.7.cloned.1.call-start = ((), (), s32[]{:S(2)}) async-start(), calls=%async_computation.6 | async-start | bytes 4718592 | tf_op jit(solution)/shard_map/reduce_scatter | solution.py:176
  362.3 236.6 %reduce-scatter.11.cloned.1.call-start = ((), (), s32[]{:S(2)}) async-start(), calls=%async_computation.9 | async-start | bytes 1437696 | tf_op jit(solution)/shard_map/reduce_scatter | solution.py:219
  415.2 10.5 copy-start.6
  474.5 8.5 copy-start.5
  540.4 10.3 copy-start.74
  554.4 14.9 %copy-start.78 = (bf16[1536,768]{1,0:T(8,128)(2,1)S(1)}, bf16[1536,768]{1,0:T(8,128)(2,1)}, u32[]{:S(2)}) copy-start(bf16[1536,768]{1,0:T(8,128)(2,1)} %param.11) | copy-start | bytes 7077892
  579.3 269.9 %all-reduce.5.cloned.1.call-start = ((), (), s32[]{:S(2)}) async-start(), calls=%async_computation.10 | async-start | bytes 15216640
  579.4 11.9 %copy-start.41 = (bf16[312,768]{1,0:T(8,128)(2,1)S(1)}, bf16[312,768]{1,0:T(8,128)(2,1)}, u32[]{:S(2)}) copy-start(bf16[312,768]{1,0:T(8,128)(2,1)} %add_convert_fusion.3) | copy-start | bytes 1437700
  667.4 393.1 %all-reduce.7.cloned.1.call-start = ((), (), s32[]{:S(2)}) async-start(), calls=%async_computation.11 | async-start | bytes 21241856 | tf_op jit(solution)/shard_map/psum | solution.py:258
  668.7 8.3 copy-start.76
  (65 other events, 230.3 us)
Sparse Core Ops, SparseCore 0:
  74.7 31.3 reduce-scatter.4
  235.4 44.9 all-gather.2
  282.0 44.9 all-gather.4
  348.7 43.3 reduce-scatter.8
  394.2 43.3 reduce-scatter.6
  579.4 19.3 reduce-scatter.10
  667.5 181.6 all-reduce.4
  854.2 206.2 all-reduce.6
where the time goes:
time: 1090 us; the launch traced here: 1080 us
  waiting for transfers between devices  463 us (42%)
  local copies, waits for them, and re-layouts  276 us (25%)
  matrix products  229 us (21%)
  other arithmetic  69.3 us (6%)
  blocking collectives  28.2 us (3%)
  between operations  15.9 us (1%)
    psum x1, waiting for transfers between devices, shards(): lax.psum(shard_grad, 'clips').astype(jnp.float32)  201 us
    unnamed x9, waiting for transfers between devices  159 us
    dot_general x8, matrix products, matmul(): return jnp.dot(left, right, preferred_element_type=jnp.float32)  72.4 us
    unnamed x193, local copies, waits for them, and re-layouts  60 us
    all_gather x1, waiting for transfers between devices, shards(): rows_all = lax.all_gather(dec_in2, 'mlp', axis=0, tiled=True)  44.3 us
    dot_general x9, matrix products, transposed(): lax.dot_general(left, right, (((0,), (0,)), ((), ())), preferred_element_...  39.4 us
    dot_general x9, matrix products, against(): lax.dot_general(left, right, (((1,), (1,)), ((), ())), preferred_element_...  37.3 us
    reshape x4, local copies, waits for them, and re-layouts, to_windows(): source.reshape(-1, LONG_FRAMES // WIN, WIN, FREQ // WIN, WIN, head_count,...  32.4 us
  transfers between devices with their start and end apart: 8, of which 7 were waited for; matrix products, arithmetic and copies ran while one was open for 23% of the time, Pallas kernels for 0%

commit v1 on v0

v1 whole, which is shorter than its diff:
```python
import math

import jax
import jax.numpy as jnp
from jax import lax
from jax.experimental import pallas as pl
from jax.experimental.pallas import tpu as pltpu
from jax.sharding import PartitionSpec as P

D = 768
HEADS = 12
DD = 512
DHEADS = 16
FREQ = 8
WIN = 4
ROWS = 1536
VIS = 312
PAD = 320
SHORT_PATCHES = 512
PARAMS = 3804160
EPSILON = 1e-06
BLOCK = 256
GROUP = WIN * FREQ
HALF = DD // 2
ENC_SCALE = 1.0 / math.sqrt(D // HEADS)
DEC_SCALE = 1.0 / math.sqrt(DD // DHEADS)
LOWEST = -1e30
CORES = 2
bf16 = jnp.bfloat16
f32 = jnp.float32


def mm(left, right):
    return jnp.dot(left, right, preferred_element_type=f32)


def mm_nt(left, right):
    return lax.dot_general(left, right, (((1,), (1,)), ((), ())), preferred_element_type=f32)


def mm_tn(left, right):
    return lax.dot_general(left, right, (((0,), (0,)), ((), ())), preferred_element_type=f32)


def normalize(rows):
    centred = rows - jnp.mean(rows, axis=-1, keepdims=True)
    scale = lax.rsqrt(jnp.mean(centred * centred, axis=-1, keepdims=True) + EPSILON)
    return centred * scale, scale


def norm_back(grad, normed, scale, gain):
    weighted = grad * gain
    return scale * (
        weighted
        - jnp.mean(weighted, axis=-1, keepdims=True)
        - normed * jnp.mean(weighted * normed, axis=-1, keepdims=True)
    )


def gelu_parts(pre):
    cdf = 0.5 * (1.0 + lax.erf(pre * math.sqrt(0.5)))
    return pre * cdf, cdf + pre * jnp.exp(-0.5 * pre * pre) * (1.0 / math.sqrt(2.0 * math.pi))


def gained(grad, normed):
    return jnp.sum(grad * normed, axis=0, keepdims=True)


SMEM = pl.BlockSpec(memory_space=pltpu.SMEM)
VMEM = pl.BlockSpec(memory_space=pltpu.VMEM)


def call(body, outs, *args, **more):
    return pl.pallas_call(
        body,
        out_shape=[jax.ShapeDtypeStruct(shape, dtype) for shape, dtype in outs],
        compiler_params=pltpu.CompilerParams(vmem_limit_bytes=56 * 2**20),
        **more,
    )(*args)


TILES = {"wqkv": 18, "wproj": 6, "wemb": 4, "wdqkv": 12, "wdproj": 4}
G1_AT = (D * 3 * D + D * D) // 128
WEMB_AT = G1_AT + 12
MASK_AT = WEMB_AT + D * 4
WDQKV_AT = MASK_AT + 4
WDPROJ_AT = WDQKV_AT + DD * 12
GD1_AT = WDPROJ_AT + DD * 4
FLAT_ROWS = PARAMS // 128
DEC_ROWS = FLAT_ROWS - WEMB_AT
PREP = 64


def widen(flat_ref, first, out_ref, tiles):
    for t in range(tiles):
        out_ref[:, t * 128 : t * 128 + 128] = flat_ref[
            pl.ds(first + t, out_ref.shape[0], stride=tiles), :
        ].astype(bf16)


def vector(flat_ref, first, count):
    return jnp.concatenate([flat_ref[first + i : first + i + 1, :] for i in range(count)], axis=1)


def flatten(flat_ref, first, value, tiles):
    for t in range(tiles):
        flat_ref[pl.ds(first + t, value.shape[0], stride=tiles), :] = value[:, t * 128 : t * 128 + 128]


def enc_prep_kernel(qkv_ref, proj_ref, gains_ref, wqkv_ref, wproj_ref, g1_ref, g2_ref, qkv_flat, proj_flat, gains_flat):
    qkv_flat[...] = qkv_ref[...].astype(f32)
    proj_flat[...] = proj_ref[...].astype(f32)
    widen(qkv_flat, 0, wqkv_ref, 18)
    widen(proj_flat, 0, wproj_ref, 6)

    @pl.when(pl.program_id(0) == 0)
    def _():
        gains_flat[...] = gains_ref[...].astype(f32)
        g1_ref[...] = vector(gains_flat, 0, 6)
        g2_ref[...] = vector(gains_flat, 6, 6)


def enc_prep(flat):
    whole = lambda *shape: pl.BlockSpec(shape, lambda i: (0,) * len(shape))
    return pl.pallas_call(
        enc_prep_kernel,
        grid=(D // PREP,),
        in_specs=[
            pl.BlockSpec((PREP * 18, 128), lambda i: (i, 0)),
            pl.BlockSpec((PREP * 6, 128), lambda i: (D * 18 // (PREP * 6) + i, 0)),
            pl.BlockSpec((16, 128), lambda i: (G1_AT // 16, 0)),
        ],
        out_specs=[
            pl.BlockSpec((PREP, 3 * D), lambda i: (i, 0)),
            pl.BlockSpec((PREP, D), lambda i: (i, 0)),
            whole(1, D),
            whole(1, D),
        ],
        out_shape=[
            jax.ShapeDtypeStruct((D, 3 * D), bf16),
            jax.ShapeDtypeStruct((D, D), bf16),
            jax.ShapeDtypeStruct((1, D), f32),
            jax.ShapeDtypeStruct((1, D), f32),
        ],
        scratch_shapes=[
            pltpu.VMEM((PREP * 18, 128), f32), pltpu.VMEM((PREP * 6, 128), f32), pltpu.VMEM((16, 128), f32),
        ],
    )(flat, flat, flat)


def dec_prep_kernel(
    flat_ref, _, wemb_ref, mask_ref, wdqkv_ref, wdproj_ref, gd1_ref, gd2_ref, low, wide, sem,
):
    copy = pltpu.make_async_copy(flat_ref.at[pl.ds(G1_AT, FLAT_ROWS - G1_AT), :], low, sem)
    copy.start()
    copy.wait()
    wide[...] = low[...].astype(f32)
    widen(wide, WEMB_AT - G1_AT, wemb_ref, 4)
    widen(wide, WDQKV_AT - G1_AT, wdqkv_ref, 12)
    widen(wide, WDPROJ_AT - G1_AT, wdproj_ref, 4)
    mask_ref[...] = vector(wide, MASK_AT - G1_AT, 4)
    gd1_ref[...] = vector(wide, GD1_AT - G1_AT, 4)
    gd2_ref[...] = vector(wide, GD1_AT - G1_AT + 4, 4)


def dec_prep(flat, after):
    hbm = pl.BlockSpec(memory_space=pl.ANY)
    return call(
        dec_prep_kernel,
        [((D, DD), bf16), ((1, DD), f32), ((DD, 3 * DD), bf16), ((DD, DD), bf16), ((1, DD), f32), ((1, DD), f32)],
        flat, after,
        in_specs=[hbm, hbm],
        scratch_shapes=[
            pltpu.VMEM((FLAT_ROWS - G1_AT, 128), bf16), pltpu.VMEM((FLAT_ROWS - G1_AT, 128), f32),
            pltpu.SemaphoreType.DMA,
        ],
    )


def enc_attend_kernel(
    x_ref, wqkv_ref, wproj_ref, g1_ref, g2_ref, segr_ref, segc_ref,
    qkv_ref, probs_ref, mix_ref, first_ref, in2_ref,
):
    x = x_ref[...].astype(f32)
    normed, _ = normalize(x)
    qkv_ref[...] = mm((normed * g1_ref[...]).astype(bf16), wqkv_ref[...]).astype(bf16)
    allowed = segr_ref[...] == segc_ref[...]
    low_lanes = lax.broadcasted_iota(jnp.int32, (PAD, 128), 1) < 64
    for pair in range(HEADS // 2):
        at = slice(pair * 128, pair * 128 + 128)
        query = qkv_ref[:, at]
        key = qkv_ref[:, D + pair * 128 : D + pair * 128 + 128]
        value = qkv_ref[:, 2 * D + pair * 128 : 2 * D + pair * 128 + 128]
        mixed = []
        for side in range(2):
            mine = low_lanes if side == 0 else jnp.logical_not(low_lanes)
            own = jnp.where(mine, query.astype(f32), 0.0).astype(bf16)
            scores = jnp.where(allowed, mm_nt(own, key) * ENC_SCALE, LOWEST)
            top = jnp.max(scores, axis=-1, keepdims=True)
            raised = jnp.exp(scores - top)
            probs = (raised / jnp.sum(raised, axis=-1, keepdims=True)).astype(bf16)
            probs_ref[2 * pair + side] = probs
            mixed.append(mm(probs, value))
        mix_ref[:, at] = jnp.where(low_lanes, mixed[0], mixed[1]).astype(bf16)
    first = x + mm(mix_ref[...], wproj_ref[...])
    first_ref[...] = first
    normed2, _ = normalize(first)
    in2_ref[...] = (normed2 * g2_ref[...]).astype(bf16)


def enc_ffn_kernel(in2_ref, fc1_ref, fc2_ref, part_ref, hidden_ref, slope_ref):
    act, slope = gelu_parts(mm(in2_ref[...], fc1_ref[...]))
    hidden = act.astype(bf16)
    hidden_ref[...] = hidden
    slope_ref[...] = slope.astype(bf16)
    part_ref[...] = mm(hidden, fc2_ref[...]).astype(part_ref.dtype)


def enc_ffn_back_kernel(out_grad_ref, slope_ref, fc1_ref, fc2_ref, pre_grad_ref, part_ref):
    grad = mm_nt(out_grad_ref[...], fc2_ref[...]) * slope_ref[...].astype(f32)
    pre_grad = grad.astype(bf16)
    pre_grad_ref[...] = pre_grad
    part_ref[...] = mm_nt(pre_grad, fc1_ref[...]).astype(part_ref.dtype)


def halve(core, value, keep_ref, send_ref):
    half = value.shape[0] // 2
    low, high = value[:half].astype(bf16), value[half:].astype(bf16)

    @pl.when(core == 0)
    def _():
        keep_ref[...] = low.reshape(keep_ref.shape)
        send_ref[...] = high.reshape(send_ref.shape)

    @pl.when(core != 0)
    def _():
        keep_ref[...] = high.reshape(keep_ref.shape)
        send_ref[...] = low.reshape(send_ref.shape)


def enc_weights_kernel(count):
    def body(core_ref, *refs):
        in2s, pre_grads, hiddens, out_grads = (refs[i * count : (i + 1) * count] for i in range(4))
        one_keep, one_send, two_keep, two_send = refs[4 * count :]
        one = mm_tn(in2s[0][...], pre_grads[0][...])
        for i in range(1, count):
            one = one + mm_tn(in2s[i][...], pre_grads[i][...])
        halve(core_ref[0], one, one_keep, one_send)
        two = mm_tn(hiddens[0][...], out_grads[0][...])
        for i in range(1, count):
            two = two + mm_tn(hiddens[i][...], out_grads[i][...])
        halve(core_ref[0], two, two_keep, two_send)

    return body


def embed_kernel(count):
    def body(first_ref, own_ref, *refs):
        parts = refs[: count - 1]
        wemb_ref, mask_ref, gd1_ref, wdqkv_ref, second_ref, table_ref, norm_ref = refs[count - 1 :]
        second = first_ref[...] + own_ref[...]
        for part in parts:
            second += part[...].astype(f32)
        low = second.astype(bf16)
        second_ref[...] = low
        embedded = mm(low, wemb_ref[...]).astype(bf16).astype(f32)
        row = lax.broadcasted_iota(jnp.int32, (PAD, DD), 0)
        start = jnp.where(row == VIS, mask_ref[...], embedded)
        normed, _ = normalize(start)
        dec_norm = (normed * gd1_ref[...]).astype(bf16)
        norm_ref[...] = dec_norm
        table_ref[:, : 3 * DD] = mm(dec_norm, wdqkv_ref[...]).astype(bf16)
        table_ref[:, 3 * DD :] = start.astype(bf16)

    return body


def spread(rows, same):
    left = jnp.concatenate([rows[:, :128]] * 4, axis=0) * same
    right = jnp.concatenate([rows[:, 128:]] * 4, axis=0) * same
    none = jnp.zeros_like(left)
    return jnp.concatenate(
        [jnp.concatenate([left, none], axis=1), jnp.concatenate([none, right], axis=1)], axis=0
    )


def segment_max(rows):
    tiles = []
    lane = lax.broadcasted_iota(jnp.int32, (rows.shape[0], 128), 1)
    for t in range(rows.shape[1] // 128):
        tile = rows[:, t * 128 : t * 128 + 128]
        for step in (1, 2, 8, 16):
            other = jnp.where(
                lane & step == 0, pltpu.roll(tile, 128 - step, 1), pltpu.roll(tile, step, 1)
            )
            tile = jnp.maximum(tile, other)
        tiles.append(tile)
    return jnp.concatenate(tiles, axis=1)


def decoder_kernel(chunks):
    def body(
        vis_ref, table_ref, cot_ref, wdproj_ref, gd2_ref, up_ref, down_ref,
        decoded_ref, up_grad_ref, down_grad_ref, proj_grad_ref, gd2_grad_ref, packed_ref,
        qkv_ref, mix_ref, s_ref, p_ref, l_ref, dmix_ref, ds_ref, d_ref, back_ref, same_ref, ones_ref,
        up_acc, down_acc, proj_acc, gd2_acc, packed_acc,
    ):
        step = pl.program_id(0)

        @pl.when(step == 0)
        def _():
            up_acc[...] = jnp.zeros_like(up_acc)
            down_acc[...] = jnp.zeros_like(down_acc)
            proj_acc[...] = jnp.zeros_like(proj_acc)
            gd2_acc[...] = jnp.zeros_like(gd2_acc)
            packed_acc[...] = jnp.zeros_like(packed_acc)
            head_row = lax.broadcasted_iota(jnp.int32, (HALF, HALF), 0) // GROUP
            head_lane = lax.broadcasted_iota(jnp.int32, (HALF, HALF), 1) // GROUP
            ones = (head_row == head_lane).astype(f32).astype(bf16)
            ones_ref[...] = ones
            same_ref[...] = ones[:128, :128]

        row = lax.broadcasted_iota(jnp.int32, (BLOCK, PAD), 0) + step * BLOCK
        named = row == vis_ref[...]
        col = lax.broadcasted_iota(jnp.int32, (BLOCK, PAD), 1)
        hit = jnp.max(jnp.where(named, 1.0, 0.0), axis=1, keepdims=True)
        one_hot = jnp.where(named, 1.0, jnp.where(col == VIS, 1.0 - hit, 0.0)).astype(bf16)
        qkv_ref[...] = mm(one_hot, table_ref[:, : 3 * DD]).astype(bf16)
        start = mm(one_hot, table_ref[:, 3 * DD :])

        lane = lax.broadcasted_iota(jnp.int32, (BLOCK, DD), 1)
        line = lax.broadcasted_iota(jnp.int32, (BLOCK, DD), 0)
        window = (lane % FREQ) // WIN == (line % FREQ) // WIN
        n_groups = BLOCK // GROUP

        def parts(group, half):
            at = pl.ds(pl.multiple_of(group * GROUP, GROUP), GROUP)
            return at, slice(half * HALF, (half + 1) * HALF)

        def scores(group, _):
            same = same_ref[...]
            for half in range(2):
                at, cols = parts(group, half)
                key = qkv_ref[at, DD + half * HALF : DD + (half + 1) * HALF]
                s_ref[at, cols] = mm_nt(qkv_ref[at, cols], spread(key, same))
            return 0

        lax.fori_loop(0, n_groups, scores, 0, unroll=4)
        raw = s_ref[...] * DEC_SCALE
        top = segment_max(raw)
        raised = jnp.where(window, jnp.exp(raw - top), 0.0)
        p_low = raised.astype(bf16)
        total = jnp.concatenate(
            [mm(p_low[:, :HALF], ones_ref[...]), mm(p_low[:, HALF:], ones_ref[...])], axis=1
        )
        l_ref[...] = top + jnp.log(total)
        p_ref[...] = (raised / total).astype(bf16)

        def mixes(group, _):
            same = same_ref[...]
            for half in range(2):
                at, cols = parts(group, half)
                value = qkv_ref[at, 2 * DD + half * HALF : 2 * DD + (half + 1) * HALF]
                mix_ref[at, cols] = mm(p_ref[at, cols], spread(value, same)).astype(bf16)
            return 0

        lax.fori_loop(0, n_groups, mixes, 0, unroll=4)

        middle = start + mm(mix_ref[...], wdproj_ref[...])
        normed, scale = normalize(middle)
        in2 = (normed * gd2_ref[...]).astype(bf16)
        cot = cot_ref[...]
        out = jnp.zeros_like(middle)
        in2_grad = jnp.zeros_like(middle)
        for c in range(chunks):
            act, slope = gelu_parts(mm(in2, up_ref[c]))
            hidden = act.astype(bf16)
            out += mm(hidden, down_ref[c])
            pre_grad = (mm_nt(cot, down_ref[c]) * slope).astype(bf16)
            in2_grad += mm_nt(pre_grad, up_ref[c])
            down_acc[c] += mm_tn(hidden, cot)
            up_acc[c] += mm_tn(in2, pre_grad)
        decoded_ref[...] = (middle + out).astype(bf16)

        gd2_acc[...] += gained(in2_grad, normed)
        middle_grad = cot.astype(f32) + norm_back(in2_grad, normed, scale, gd2_ref[...])
        branch = middle_grad.astype(bf16)
        back_ref[:, 3 * DD :] = branch
        proj_acc[...] += mm_tn(mix_ref[...], branch)
        dmix_ref[...] = mm_nt(branch, wdproj_ref[...]).astype(bf16)

        def prob_grads(group, _):
            same = same_ref[...]
            for half in range(2):
                at, cols = parts(group, half)
                value = qkv_ref[at, 2 * DD + half * HALF : 2 * DD + (half + 1) * HALF]
                s_ref[at, cols] = mm_nt(dmix_ref[at, cols], spread(value, same))
            return 0

        lax.fori_loop(0, n_groups, prob_grads, 0, unroll=4)
        probs = p_ref[...].astype(f32)
        prob_grad = s_ref[...]
        weighed = (probs * prob_grad).astype(bf16)
        row_sum = jnp.concatenate(
            [mm(weighed[:, :HALF], ones_ref[...]), mm(weighed[:, HALF:], ones_ref[...])], axis=1
        )
        d_ref[...] = row_sum
        ds_ref[...] = (probs * (prob_grad - row_sum)).astype(bf16)

        small_lane = lax.broadcasted_iota(jnp.int32, (GROUP, HALF), 1)
        small_line = lax.broadcasted_iota(jnp.int32, (GROUP, HALF), 0)
        pick = small_lane % GROUP == small_line
        small_window = (small_lane % FREQ) // WIN == (small_line % FREQ) // WIN

        def qkv_grads(group, _):
            same = same_ref[...]
            for half in range(2):
                at, cols = parts(group, half)
                key_cols = slice(DD + half * HALF, DD + (half + 1) * HALF)
                value_cols = slice(2 * DD + half * HALF, 2 * DD + (half + 1) * HALF)
                key = qkv_ref[at, key_cols]
                wide_query = spread(qkv_ref[at, cols], same)
                wide_mix_grad = spread(dmix_ref[at, cols], same)
                back_ref[at, cols] = (mm(ds_ref[at, cols], spread(key, same)) * DEC_SCALE).astype(bf16)
                log_total = jnp.sum(jnp.where(pick, l_ref[at, cols], 0.0), axis=0, keepdims=True)
                turned_sum = jnp.sum(jnp.where(pick, d_ref[at, cols], 0.0), axis=0, keepdims=True)
                turned = mm_nt(key, wide_query) * DEC_SCALE
                turned = jnp.where(small_window, jnp.exp(turned - log_total), 0.0)
                turned_grad = mm_nt(qkv_ref[at, value_cols], wide_mix_grad)
                score_grad = (turned * (turned_grad - turned_sum)).astype(bf16)
                back_ref[at, key_cols] = (mm(score_grad, wide_query) * DEC_SCALE).astype(bf16)
                back_ref[at, value_cols] = mm(turned.astype(bf16), wide_mix_grad).astype(bf16)
            return 0

        lax.fori_loop(0, n_groups, qkv_grads, 0, unroll=2)
        packed_acc[...] += mm_tn(one_hot, back_ref[...])

        @pl.when(step == pl.num_programs(0) - 1)
        def _():
            up_grad_ref[...] = up_acc[...].astype(bf16)
            down_grad_ref[...] = down_acc[...].astype(bf16)
            proj_grad_ref[...] = proj_acc[...].astype(bf16)
            gd2_grad_ref[...] = gd2_acc[...]
            packed_ref[...] = packed_acc[...]

    return body


def decoder(vis_row, table, cotangent, w_dproj, gd_two, up, down):
    chunks, _, width = up.shape
    rows = cotangent.shape[0]
    kept = lambda *shape: pl.BlockSpec(shape, lambda i: (0,) * len(shape), pipeline_mode=pl.Buffered(1))
    by_rows = pl.BlockSpec((BLOCK, DD), lambda i: (i, 0))
    outs = [
        ((rows, DD), bf16, by_rows),
        ((chunks, DD, width), bf16, kept(chunks, DD, width)),
        ((chunks, width, DD), bf16, kept(chunks, width, DD)),
        ((DD, DD), bf16, kept(DD, DD)),
        ((1, DD), f32, kept(1, DD)),
        ((PAD, 4 * DD), f32, kept(PAD, 4 * DD)),
    ]
    return pl.pallas_call(
        decoder_kernel(chunks),
        grid=(rows // BLOCK,),
        in_specs=[
            kept(1, PAD), kept(PAD, 4 * DD), by_rows, kept(DD, DD), kept(1, DD),
            kept(chunks, DD, width), kept(chunks, width, DD),
        ],
        out_specs=[spec for _, _, spec in outs],
        out_shape=[jax.ShapeDtypeStruct(shape, dtype) for shape, dtype, _ in outs],
        scratch_shapes=[
            pltpu.VMEM((BLOCK, 3 * DD), bf16),
            pltpu.VMEM((BLOCK, DD), bf16),
            pltpu.VMEM((BLOCK, DD), f32),
            pltpu.VMEM((BLOCK, DD), bf16),
            pltpu.VMEM((BLOCK, DD), f32),
            pltpu.VMEM((BLOCK, DD), bf16),
            pltpu.VMEM((BLOCK, DD), bf16),
            pltpu.VMEM((BLOCK, DD), f32),
            pltpu.VMEM((BLOCK, 4 * DD), bf16),
            pltpu.VMEM((128, 128), bf16),
            pltpu.VMEM((HALF, HALF), bf16),
            pltpu.VMEM((chunks, DD, width), f32),
            pltpu.VMEM((chunks, width, DD), f32),
            pltpu.VMEM((DD, DD), f32),
            pltpu.VMEM((1, DD), f32),
            pltpu.VMEM((PAD, 4 * DD), f32),
        ],
        compiler_params=pltpu.CompilerParams(vmem_limit_bytes=56 * 2**20),
    )(vis_row, table, cotangent, w_dproj, gd_two, up, down)


def embed_back_kernel(
    packed_ref, table_ref, norm_ref, second_ref, gd1_ref, wdqkv_ref, wemb_ref,
    second_grad_ref, out_grad_ref, qkv_grad_ref, embed_grad_ref, gd1_grad_ref, mask_grad_ref,
):
    qkv_grad = packed_ref[:, : 3 * DD].astype(bf16)
    qkv_grad_ref[...] = qkv_grad
    grad = mm_nt(qkv_grad, wdqkv_ref[...])
    normed, scale = normalize(table_ref[:, 3 * DD :].astype(f32))
    gd1_grad_ref[...] = gained(grad, normed)
    start_grad = packed_ref[:, 3 * DD :] + norm_back(grad, normed, scale, gd1_ref[...])
    mask_grad_ref[...] = start_grad[VIS : VIS + 1]
    row = lax.broadcasted_iota(jnp.int32, (PAD, DD), 0)
    embed_grad = jnp.where(row < VIS, start_grad, 0.0).astype(bf16)
    embed_grad_ref[...] = embed_grad
    second_grad = mm_nt(embed_grad, wemb_ref[...])
    second_grad_ref[...] = second_grad
    out_grad_ref[...] = second_grad.astype(bf16)


def dec_flat_kernel(
    norm_ref, qkv_grad_ref, second_ref, embed_grad_ref, proj_grad_ref, mask_grad_ref, gd1_grad_ref, gd2_grad_ref,
    flat_ref, wide,
):
    flatten(wide, 0, mm_tn(second_ref[...], embed_grad_ref[...]), 4)
    flatten(wide, MASK_AT - WEMB_AT, mask_grad_ref[...], 4)
    flatten(wide, WDQKV_AT - WEMB_AT, mm_tn(norm_ref[...], qkv_grad_ref[...]), 12)
    flatten(wide, WDPROJ_AT - WEMB_AT, proj_grad_ref[...].astype(f32), 4)
    flatten(wide, GD1_AT - WEMB_AT, gd1_grad_ref[...], 4)
    flatten(wide, GD1_AT + 4 - WEMB_AT, gd2_grad_ref[...], 4)
    flat_ref[...] = wide[...].astype(bf16)


def enc_back_kernel(count, ring):
    def body(core_ref, own_ref, *refs):
        parts = refs[: count - 1]
        (
            second_grad_ref, first_ref, x_ref, qkv_ref, probs_ref, mix_ref, wqkv_ref, wproj_ref, g1_ref, g2_ref,
            dec_flat_ref, input_grad_ref, keep_ref, send_ref, qkv_grad_ref, wide,
        ) = refs[count - 1 :]
        in2_grad = own_ref[...]
        for part in parts:
            in2_grad += part[...].astype(f32)
        normed2, scale2 = normalize(first_ref[...])
        flatten(wide, G1_AT + 6, gained(in2_grad, normed2), 6)
        first_grad = second_grad_ref[...] + norm_back(in2_grad, normed2, scale2, g2_ref[...])
        branch = first_grad.astype(bf16)
        flatten(wide, D * 18, mm_tn(mix_ref[...], branch), 6)
        wide[WEMB_AT:, :] = dec_flat_ref[...].astype(f32)
        mix_grad = mm_nt(branch, wproj_ref[...]).astype(bf16)
        low_lanes = lax.broadcasted_iota(jnp.int32, (PAD, 128), 1) < 64
        for pair in range(HEADS // 2):
            at = slice(pair * 128, pair * 128 + 128)
            query = qkv_ref[:, at]
            key = qkv_ref[:, D + pair * 128 : D + pair * 128 + 128]
            value = qkv_ref[:, 2 * D + pair * 128 : 2 * D + pair * 128 + 128]
            upstream = mix_grad[:, at]
            found = []
            for side in range(2):
                mine = low_lanes if side == 0 else jnp.logical_not(low_lanes)
                own = jnp.where(mine, upstream.astype(f32), 0.0).astype(bf16)
                low_probs = probs_ref[2 * pair + side]
                probs = low_probs.astype(f32)
                prob_grad = mm_nt(own, value)
                row_sum = jnp.sum(probs * prob_grad, axis=-1, keepdims=True)
                score_grad = (probs * (prob_grad - row_sum)).astype(bf16)
                found.append((mm(score_grad, key), mm_tn(score_grad, query), mm_tn(low_probs, upstream)))
            for part, factor in enumerate((ENC_SCALE, ENC_SCALE, 1.0)):
                merged = jnp.where(low_lanes, found[0][part], found[1][part]) * factor
                qkv_grad_ref[:, part * D + pair * 128 : part * D + pair * 128 + 128] = merged.astype(bf16)
        normed, scale = normalize(x_ref[...].astype(f32))
        flatten(wide, 0, mm_tn((normed * g1_ref[...]).astype(bf16), qkv_grad_ref[...]), 18)
        grad = mm_nt(qkv_grad_ref[...], wqkv_ref[...])
        flatten(wide, G1_AT, gained(grad, normed), 6)
        input_grad_ref[...] = (first_grad + norm_back(grad, normed, scale, g1_ref[...]))[:VIS]

        part = FLAT_ROWS // ring.group
        height = keep_ref.shape[3]

        def split(target, half):
            for way in range(2):
                for chip in range(ring.chips):
                    first = ((half * 2 + way) * ring.chips + chip) * height
                    for y in range(ring.group):
                        count = min(height, part - first)
                        if count > 0:
                            target[way, chip, y, :count] = wide[y * part + first : y * part + first + count, :].astype(bf16)
                        if count < height:
                            target[way, chip, y, max(count, 0) :] = jnp.zeros((height - max(count, 0), 128), bf16)

        for half in range(CORES):
            @pl.when(core_ref[0] == half)
            def _(half=half):
                split(keep_ref, half)
                split(send_ref, 1 - half)

    return body


class Ring:
    def __init__(self, clips, group):
        self.chips = clips // CORES
        self.group = group
        chips = self.chips
        if chips == 8:
            order = [4 * z // 2 for z in range(4)] + [4 * z // 2 + 1 for z in reversed(range(4))]
        else:
            order = list(range(chips))
        place = [0] * chips
        for at, chip in enumerate(order):
            place[chip] = at
        clip = lax.axis_index("clips")
        self.core = clip % CORES
        chip = clip // CORES
        if chips == 8:
            self.at = jnp.where(chip % 2 == 0, chip // 2, 7 - chip // 2)
        else:
            self.at = chip
        self.lane = lax.axis_index("mlp")
        step = lambda way: [
            (order[i] * CORES + c, order[(i + way) % chips] * CORES + c) for i in range(chips) for c in range(CORES)
        ]
        self.ways = (step(1), step(-1))
        self.swap = [(i, i ^ 1) for i in range(clips)]
        self.clips = clips

    def clip_of(self, side, slot):
        chip = jnp.where(slot < 4, 2 * slot, 15 - 2 * slot) if self.chips == 8 else slot
        return chip * CORES + side


    def fetch(self, block):
        half = block.shape[0] // CORES
        mine = lax.dynamic_slice_in_dim(block, self.core * half, half, 0)
        blocks = [block]
        for k in range(1, self.group):
            near = lax.ppermute(mine, "mlp", [(j, (j - k) % self.group) for j in range(self.group)])
            far = self.swapped(near)
            low, high = (jnp.where(self.core == side, near, far) for side in range(CORES))
            blocks.append(jnp.concatenate([low, high]))
        stacked = jnp.stack(blocks)
        if self.group == 2:
            return jnp.where(self.lane == 0, stacked, stacked[::-1])
        return jnp.roll(stacked, self.lane, axis=0)

    def halves(self, rows, width):
        return ((2, self.chips, rows // (2 * CORES * self.chips), width), bf16)

    def swapped(self, value):
        return lax.ppermute(value, "clips", self.swap)

    def block(self, half, way, back):
        sign = 1 if way == 0 else -1
        return lax.dynamic_index_in_dim(half[way], (self.at - sign * back) % self.chips, 0, False)

    def scattered(self, grads):
        group, rows, width = grads.shape
        blocks = grads.reshape(group, self.clips, rows // self.clips, width).transpose(1, 0, 2, 3)
        flat = blocks.reshape(-1, width)
        return lax.psum_scatter(flat, "clips", scatter_dimension=0, tiled=True).reshape(group, -1, width)

    def scattered_trip(self, block):
        group, rows, width = block.shape
        ways = block.reshape(group, 2, rows // 2, width)
        held = yield self.over_group([ways[:, 0], ways[:, 1]])
        return (yield from self.spread(held))

    def scattered_row(self, rows):
        height = rows // (self.clips * 2)
        return lambda side, way, slot: (self.clip_of(side, slot) * 2 + way) * height

    def start(self, keep, send):
        return keep + self.swapped(send)

    def round_trip(self, half):
        held = [self.block(half, way, 0) for way in range(2)]
        for step in range(1, self.chips):
            came = [lax.ppermute(held[way], "clips", self.ways[way]) for way in range(2)]
            held = yield [came[way] + self.block(half, way, step) for way in range(2)]
        if half.ndim == 5:
            held = yield self.over_group(held)
        return (yield from self.spread(held))

    def over_group(self, held):
        both = jnp.stack(held, axis=1)
        total = lax.dynamic_index_in_dim(both, self.lane, 0, False)
        for k in range(1, self.group):
            away = lax.dynamic_index_in_dim(both, (self.lane + k) % self.group, 0, False)
            total = total + lax.ppermute(away, "mlp", [(j, (j + k) % self.group) for j in range(self.group)])
        return [total[0], total[1]]

    def spread(self, held):
        found = [[held[0]], [held[1]]]
        cut = self.chips - 2
        early = None
        for step in range(1, self.chips):
            came = yield [lax.ppermute(found[way][-1], "clips", self.ways[way]) for way in range(2)]
            for way in range(2):
                found[way].append(came[way])
            if step == cut - 1:
                early = self.swapped(jnp.stack(found[0] + found[1]))
        late = self.swapped(jnp.stack(found[0][cut:] + found[1][cut:]))
        return found[0] + found[1], early, late


def in_step(*trips):
    done = [None] * len(trips)
    kept = [None] * len(trips)
    round_at = 0
    while any(one is None for one in done):
        live = []
        for i, (trip, first) in enumerate(trips):
            if done[i] is None and round_at >= first:
                try:
                    kept[i] = next(trip) if kept[i] is None else trip.send(kept[i])
                    live.append(i)
                except StopIteration as end:
                    done[i] = end.value
        if live:
            tied = lax.optimization_barrier([kept[i] for i in live])
            for i, value in zip(live, tied):
                kept[i] = value
        round_at += 1
    return done


def place_kernel(chips, height, total, row_of, lead):
    cut = chips - 2

    def body(where_ref, *refs):
        mine, early, late, out = refs[: 2 * chips], refs[2 * chips], refs[2 * chips + 1], refs[2 * chips + 2]
        core, at = where_ref[0], where_ref[1]

        def put(side, way, slot, value):
            row = row_of(side, way, slot)
            if total % height == 0:
                out[pl.ds(pl.multiple_of(row, 8) if height % 8 == 0 else row, height), :] = value
            else:
                short = total % height

                @pl.when(row + height <= total)
                def _():
                    out[pl.ds(pl.multiple_of(row, 8), height), :] = value

                @pl.when(row + height > total)
                def _():
                    out[total - short :, :] = value[:short]

        for way in range(2):
            sign = 1 if way == 0 else -1
            for step in range(chips):
                slot = lax.rem(at + sign * (lead - step) + chips, chips)
                put(core, way, slot, mine[way * chips + step][...].astype(f32))
                other = early[way * cut + step] if step < cut else late[way * 2 + step - cut]
                put(1 - core, way, slot, other.astype(f32))

    return body


def place_rows(ring, found, total, row_of, lead):
    mine, early, late = found
    cut = ring.chips - 2
    out = jnp.zeros((total, mine[0].shape[1]), f32)
    for way in range(2):
        for step in range(ring.chips):
            slot = (ring.at + (1 if way == 0 else -1) * (lead - step)) % ring.chips
            other = early[way * cut + step] if step < cut else late[way * 2 + step - cut]
            for side, value in ((ring.core, mine[way * ring.chips + step]), (1 - ring.core, other)):
                out = lax.dynamic_update_slice_in_dim(out, value.astype(f32), row_of(side, way, slot), 0)
    return out


def place(ring, where, found, total, row_of=None, lead=1):
    mine, early, late = found
    height, width = mine[0].shape
    if row_of is None:
        row_of = lambda side, way, slot: ((side * 2 + way) * ring.chips + slot) * height
    if height % 8:
        return place_rows(ring, found, total, row_of, lead)
    return call(
        place_kernel(ring.chips, height, total, row_of, lead),
        [((total, width), f32)],
        where, *mine, early, late,
        in_specs=[SMEM] + [VMEM] * (len(mine) + 2),
    )[0]


def after(value, *others):
    return lax.optimization_barrier((value,) + others)[0]


def shards(clips, group, flat_params, w_fc1, w_fc2, w_up, w_down, patches, clip_ids, visible_index, cotangent):
    width = w_fc1.shape[1]
    ring = Ring(clips, group)
    core = ring.core.astype(jnp.int32).reshape(1)
    turns = [[(i, (i + k) % group) for i in range(group)] for k in range(1, group)]
    back_turns = [[(i, (i - k) % group) for i in range(group)] for k in range(1, group)]

    up_all = ring.fetch(w_up)
    down_all = ring.fetch(w_down)

    flat = flat_params.reshape(FLAT_ROWS, 128)
    w_qkv, w_proj, g_one, g_two = enc_prep(flat)
    x = jnp.pad(patches, ((0, PAD - VIS), (0, 0)))
    vis = jnp.pad(visible_index, (0, PAD - VIS), constant_values=-1)
    segment = jnp.where(vis < 0, -1, jnp.minimum(vis // SHORT_PATCHES, clip_ids[ROWS - 1]))
    qkv, probs, mix, first, in2 = call(
        enc_attend_kernel,
        [((PAD, 3 * D), bf16), ((HEADS, PAD, PAD), bf16), ((PAD, D), bf16), ((PAD, D), f32), ((PAD, D), bf16)],
        x, w_qkv, w_proj, g_one, g_two, segment[None, :], segment[:, None],
    )

    in2s, hiddens, slopes, parts = [in2], [], [], []
    for i in range(group):
        if i > 0:
            in2s.append(after(lax.ppermute(in2, "mlp", turns[i - 1]), parts[0]))
        part, hidden, slope = call(
            enc_ffn_kernel,
            [((PAD, D), f32 if i == 0 else bf16), ((PAD, width), bf16), ((PAD, width), bf16)],
            in2s[i], w_fc1, w_fc2,
        )
        hiddens.append(hidden)
        slopes.append(slope)
        parts.append(part if i == 0 else lax.ppermute(part, "mlp", back_turns[i - 1]))
    w_embed, mask_token, w_dqkv, w_dproj, gd_one, gd_two = dec_prep(flat, part)

    second_low, table, dec_norm = call(
        embed_kernel(group),
        [((PAD, D), bf16), ((PAD, 4 * DD), bf16), ((PAD, DD), bf16)],
        first, *parts, w_embed, mask_token, gd_one, w_dqkv,
    )
    decoded, up_part, down_part, wdproj_grad, gd_two_grad, packed = decoder(
        vis[None, :], table, cotangent, w_dproj, gd_two, up_all, down_all
    )
    up_mine = ring.scattered(up_part)
    down_mine = ring.scattered(down_part)
    second_grad, out_grad, dec_qkv_grad, embed_grad, gd_one_grad, mask_grad = call(
        embed_back_kernel,
        [
            ((PAD, D), f32), ((PAD, D), bf16), ((PAD, 3 * DD), bf16), ((PAD, DD), bf16), ((1, DD), f32), ((1, DD), f32),
        ],
        packed, table, dec_norm, second_low, gd_one, w_dqkv, w_embed,
    )
    dec_flat = call(
        dec_flat_kernel,
        [((DEC_ROWS, 128), bf16)],
        dec_norm, dec_qkv_grad, second_low, embed_grad, wdproj_grad, mask_grad, gd_one_grad, gd_two_grad,
        scratch_shapes=[pltpu.VMEM((DEC_ROWS, 128), f32)],
    )[0]

    out_grads, pre_grads, parts = [out_grad], [], []
    for i in range(group):
        if i > 0:
            out_grads.append(after(lax.ppermute(out_grad, "mlp", turns[i - 1]), parts[0], dec_flat))
        pre_grad, part = call(
            enc_ffn_back_kernel,
            [((PAD, width), bf16), ((PAD, D), f32 if i == 0 else bf16)],
            out_grads[i], slopes[i], w_fc1, w_fc2,
        )
        pre_grads.append(pre_grad)
        parts.append(part if i == 0 else lax.ppermute(part, "mlp", back_turns[i - 1]))
    fc1_halves = ring.halves(D, width)
    fc2_halves = ring.halves(width, D)
    fc1_keep, fc1_send, fc2_keep, fc2_send = call(
        enc_weights_kernel(group), [fc1_halves, fc1_halves, fc2_halves, fc2_halves],
        core, *in2s, *pre_grads, *hiddens, *out_grads,
        in_specs=[SMEM] + [VMEM] * (4 * group),
    )
    parts[1:] = [after(part, fc1_keep) for part in parts[1:]]
    height = -(-FLAT_ROWS // group // (CORES * 2 * ring.chips) // 8) * 8
    flat_halves = ((2, ring.chips, group, height, 128), bf16)
    input_grad, flat_keep, flat_send = call(
        enc_back_kernel(group, ring),
        [((VIS, D), f32), flat_halves, flat_halves],
        core, *parts, second_grad, first, x, qkv, probs, mix, w_qkv, w_proj, g_one, g_two, dec_flat,
        in_specs=[SMEM] + [VMEM] * (group + 11),
        scratch_shapes=[pltpu.VMEM((PAD, 3 * D), bf16), pltpu.VMEM((FLAT_ROWS, 128), f32)],
    )
    fc1_found, fc2_found, flat_found, up_found, down_found = in_step(
        (ring.round_trip(ring.start(fc1_keep, fc1_send)), 0),
        (ring.round_trip(ring.start(fc2_keep, fc2_send)), 0),
        (ring.round_trip(ring.start(flat_keep, flat_send)), 2),
        (ring.scattered_trip(up_mine), ring.chips + 2),
        (ring.scattered_trip(down_mine), ring.chips + 2),
    )
    where = jnp.stack([ring.core, ring.at]).astype(jnp.int32)
    return (
        decoded,
        input_grad,
        place(ring, where, flat_found, FLAT_ROWS // group).reshape(-1),
        place(ring, where, fc1_found, D),
        place(ring, where, fc2_found, width),
        place(ring, where, up_found, DD, ring.scattered_row(DD), 0),
        place(ring, where, down_found, w_down.shape[0], ring.scattered_row(w_down.shape[0]), 0),
    )


def solution(mesh):
    placed = (
        P(),
        P(None, "mlp"),
        P("mlp", None),
        P(None, "mlp"),
        P("mlp", None),
        P(("clips", "mlp"), None),
        P(("clips", "mlp")),
        P(("clips", "mlp")),
        P(("clips", "mlp"), None),
    )
    group = mesh.shape["mlp"]

    def body(*args):
        return shards(mesh.shape["clips"], group, *args)

    return jax.shard_map(
        body,
        mesh=mesh,
        in_specs=placed,
        out_specs=(
            P(("clips", "mlp"), None),
            P(("clips", "mlp"), None),
            P("mlp"),
            P(None, "mlp"),
            P("mlp", None),
            P(None, "mlp"),
            P("mlp", None),
        ),
        check_vma=False,
    )
```

time: 1090 us -> 596 us (0.55)
  waiting for transfers between devices: 463 us -> 152 us
  matrix products: 229 us -> 0 us
  local copies, waits for them, and re-layouts: 276 us -> 55.2 us
  Pallas kernels: 0 us -> 206 us
  starting transfers between devices: 0.33 us -> 131 us
  other arithmetic: 69.3 us -> 24.7 us
  blocking collectives: 28.2 us -> 0 us
    dot_general x39 -> x0, matrix products: 229 us -> none  [the longest x8 72.4 us: matmul(): return jnp.dot(left, right, preferred_element_type=jnp.float32)]
    pallas_call x0 -> x18, Pallas kernels: none -> 206 us  [the longest x16 106 us: call(): pl.pallas_call(body, out_shape=[jax.ShapeDtypeStruct(shape, dtype) for sh...]
    psum x1 -> x0, waiting for transfers between devices: 201 us -> none  [shards(): lax.psum(shard_grad, 'clips').astype(jnp.float32)]
    unnamed x9 -> x2, waiting for transfers between devices: 159 us -> 0.03 us
    ppermute x0 -> x136, starting transfers between devices: none -> 131 us  [the longest x70 72.9 us: spread(): lax.ppermute(found[way][-1], 'clips', self.ways[way])]
    ppermute x0 -> x136, waiting for transfers between devices: none -> 100 us  [the longest x42 36.7 us: round_trip(): lax.ppermute(held[way], 'clips', self.ways[way])]
    reshape x16 -> x2, local copies, waits for them, and re-layouts: 99.7 us -> 4.74 us  [scattered(): grads.reshape(group, self.clips, rows // self.clips, width)]
    all_gather x2 -> x0, waiting for transfers between devices: 57.2 us -> none  [the longest x1 44.3 us: shards(): rows_all = lax.all_gather(dec_in2, 'mlp', axis=0, tiled=True)]
  transfers between devices with their start and end apart: 8 -> 138, of which waited for: 7 -> 51; matrix products, arithmetic and copies ran while one was open for 23% -> 11% of each run, Pallas kernels for 0% -> 15%
where the time goes in v1:
time: 596 us; the launch traced here: 586 us
  Pallas kernels  206 us (35%)
  waiting for transfers between devices  152 us (26%)
  starting transfers between devices  131 us (22%)
  local copies, waits for them, and re-layouts  55.2 us (9%)
  other arithmetic  24.7 us (4%)
  between operations  16.3 us (3%)
    pallas_call x16, Pallas kernels, call(): pl.pallas_call(body, out_shape=[jax.ShapeDtypeStruct(shape, dtype) for sh...  106 us
    pallas_call x1, Pallas kernels, decoder(): pl.pallas_call(decoder_kernel(chunks), grid=(rows // BLOCK,), in_specs=[k...  91.4 us
    ppermute x70, starting transfers between devices, spread(): lax.ppermute(found[way][-1], 'clips', self.ways[way])  72.9 us
    reduce_scatter x2, waiting for transfers between devices, scattered(): lax.psum_scatter(flat, 'clips', scatter_dimension=0, tiled=True)  51.8 us
    ppermute x42, starting transfers between devices, round_trip(): lax.ppermute(held[way], 'clips', self.ways[way])  46.2 us
    unnamed x253, local copies, waits for them, and re-layouts  36.9 us
    ppermute x42, waiting for transfers between devices, round_trip(): lax.ppermute(held[way], 'clips', self.ways[way])  36.7 us
    ppermute x70, waiting for transfers between devices, spread(): lax.ppermute(found[way][-1], 'clips', self.ways[way])  32.3 us
  transfers between devices with their start and end apart: 138, of which 51 were waited for; matrix products, arithmetic and copies ran while one was open for 11% of the time, Pallas kernels for 15%

profile of v1, /device:TPU:0, one launch (start us, length us, event | category | flops | bytes accessed | tf_op | source)
XLA Modules:
  0.0 585.8 jit_solution(1332819647581962243)
XLA Ops:
  8.3 3.0 collective-permute-start.4
  15.3 9.0 %shard_map.144 = (bf16[768,2304]{1,0:T(8,128)(2,1)}, bf16[768,768]{1,0:T(8,128)(2,1)}, f32[1,768]{1,0:T(1,128)}, f32[1,768]{1,0:T(1,128)}) custom-call(bf16[29720,128]{1,0:T(8,128)(2,1)} %bitcast.285, bf16[29720,128]{1,0:T(8,128)(2,1)} %bitcast.286, bf16[29720,128]{1,0:T(8,128)(2,1)} %bitcast.287), custom_call_target="tpu_custom_call" | custom-call | tf_op jit(solution)/shard_map/pallas_call | solution.py:125
  25.2 11.1 %shard_map.145 = (bf16[320,2304]{1,0:T(8,128)(2,1)}, bf16[12,320,320]{2,1,0:T(8,128)(2,1)}, bf16[320,768]{1,0:T(8,128)(2,1)}, f32[320,768]{1,0:T(8,128)}, bf16[320,768]{1,0:T(8,128)(2,1)}) custom-call(bf16[320,768]{1,0:T(8,128)(2,1)} %pad.9.x_ref.refs_3_, bf16[768,2304]{1,0:T(8,128)(2,1)} %get-tuple-element.175.wqkv_ref.refs_7_, ...), custom_call_target="tpu_custom_call" | custom-call | tf_op jit(solution)/shard_map/pallas_call | solution.py:74
  38.4 5.4 shard_map.146
  43.8 6.8 %collective-permute-done.in2_ref.refs_1_ = bf16[320,768]{1,0:T(8,128)(2,1)S(1)} collective-permute-done((bf16[320,768]{1,0:T(8,128)(2,1)}, bf16[320,768]{1,0:T(8,128)(2,1)S(1)}, u32[]{:S(2)}, u32[]{:S(2)}) %collective-permute-start) | collective-permute-done | bytes 491552 | tf_op jit(solution)/shard_map/ppermute | solution.py:807
  51.4 5.3 shard_map.147
  57.3 4.1 shard_map.148
  61.9 9.0 %collective-permute-done.1.refs_0_ = bf16[320,768]{1,0:T(8,128)(2,1)S(1)} collective-permute-done((bf16[320,768]{1,0:T(8,128)(2,1)}, bf16[320,768]{1,0:T(8,128)(2,1)S(1)}, u32[]{:S(2)}, u32[]{:S(2)}) %collective-permute-start.1) | collective-permute-done | bytes 491552 | tf_op jit(solution)/shard_map/ppermute | solution.py:815
  71.7 5.0 shard_map.149
  83.3 91.4 %shard_map.150 = (bf16[1536,512]{1,0:T(8,128)(2,1)}, bf16[2,512,1024]{2,1,0:T(8,128)(2,1)}, bf16[2,1024,512]{2,1,0:T(8,128)(2,1)}, bf16[512,512]{1,0:T(8,128)(2,...) custom-call(s32[1,320]{1,0:T(1,128)} %broadcast_in_dim.13.vis_ref, bf16[320,2048]{1,0:T(8,128)(2,1)} %get-tuple-element.188.table_ref, ...), custom_call_target="tpu_custom_call" | custom-call | tf_op jit(solution)/shard_map/pallas_call | solution.py:462
  174.7 5.8 shard_map.151
  180.8 5.7 shard_map.152
  186.5 5.1 shard_map.153.refs_11_
  193.3 5.5 shard_map.154
  198.8 10.7 %shard_map.155 = (bf16[2,8,24,1536]{3,2,1,0:T(8,128)(2,1)}, bf16[2,8,24,1536]{3,2,1,0:T(8,128)(2,1)}, bf16[2,8,48,768]{3,2,1,0:T(8,128)(2,1)}, bf16[2,8,48,768]{3,2,1,0:T(8,128)(2,1)}) custom-call(s32[1]{0:T(128)} %bitcast.6.core_ref, bf16[320,768]{1,0:T(8,128)(2,1)} %get-tuple-element.180.in2_ref.refs_0_, bf16[320,768]{1,0:T(8,128)(2,1)} %copy-done.7, ...), custom_call_target="tpu_custom_call" | custom-call | tf_op jit(solution)/shard_map/pallas_call | solution.py:74
  212.7 10.5 %collective-permute-done.7.refs_0_ = bf16[320,768]{1,0:T(8,128)(2,1)S(1)} collective-permute-done((bf16[320,768]{1,0:T(8,128)(2,1)S(1)}, bf16[320,768]{1,0:T(8,128)(2,1)S(1)}, u32[]{:S(2)}, u32[]{:S(2)}) %collective-permute-start.7) | collective-permute-done | bytes 491552 | tf_op jit(solution)/shard_map/ppermute | solution.py:852
  224.0 22.0 %shard_map.156 = (f32[312,768]{1,0:T(8,128)}, bf16[2,8,2,472,128]{4,3,2,1,0:T(8,128)(2,1)}, bf16[2,8,2,472,128]{4,3,2,1,0:T(8,128)(2,1)}) custom-call(s32[1]{0:T(128)} %bitcast.6.core_ref, f32[320,768]{1,0:T(8,128)} %get-tuple-element.197.own_ref, bf16[320,768]{1,0:T(8,128)(2,1)} %copy-done.20, f32[320,768]{1,0:T(8,128)} %get-tuple-element.213.refs_1_, ...), custom_call_target="tpu_custom_call" | custom-call | tf_op jit(solution)/shard_map/pallas_call | solution.py:74
  251.0 6.0 %collective-permute-done.10 = bf16[24,1536]{1,0:T(8,128)(2,1)S(1)} collective-permute-done((bf16[24,1536]{1,0:T(8,128)(2,1)S(1)}, bf16[24,1536]{1,0:T(8,128)(2,1)S(1)}, u32[]{:S(2)}, u32[]{:S(2)}) %collective-permute-start.10) | collective-permute-done | bytes 73760 | tf_op jit(solution)/shard_map/ppermute | solution.py:669
  259.0 3.2 copy.17
  264.5 3.4 collective-permute-done.17
  278.8 4.3 add.396
  290.4 51.8 %reduce-scatter.3.cloned.1.call-done = bf16[64,1024]{1,0:T(8,128)(2,1)} async-done(((bf16[1024,1024]{1,0:T(8,128)(2,1)}), bf16[64,1024]{1,0:T(8,128)(2,1)}) %reduce-scatter.3.cloned.1.call-update) | async-done | bytes 131088 | tf_op jit(solution)/shard_map/reduce_scatter | solution.py:651
  354.3 2.9 collective-permute-done.25
  358.9 3.6 collective-permute-done.27
  369.7 4.9 collective-permute-done.31
  383.4 3.6 collective-permute-done.37
  397.0 4.8 collective-permute-done.43
  458.0 4.1 collective-permute-done.75.refs_13_
  553.7 2.8 shard_map.161
  560.4 4.2 shard_map.159
  566.2 4.2 shard_map.158
  572.3 6.2 %shard_map.157 = f32[14860,128]{1,0:T(8,128)} custom-call(s32[2]{0:T(128)} %pad_add_fusion.where_ref, bf16[472,128]{1,0:T(8,128)(2,1)} %copy-done.13, bf16[472,128]{1,0:T(8,128)(2,1)} %copy-done.23, bf16[472,128]{1,0:T(8,128)(2,1)} %copy-done.25, bf16[472,128]{1,0:T(8,128)(2,1)} %copy-done.27, bf16[472,128]{1,0:T(8,128)(2,1)} %copy-done.29, ...), custom_call_target="tpu_custom_call" | custom-call | tf_op jit(solution)/shard_map/pallas_call | solution.py:74
  (609 shorter events, 244.2 us)
Async XLA Ops:
  7.2 278.8 %reduce-scatter.5.cloned.1.call-start = ((), (), s32[]{:S(2)}) async-start(), calls=%async_computation.3 | async-start | bytes 2228224 | tf_op jit(solution)/shard_map/reduce_scatter | solution.py:651
  8.3 30.1 %collective-permute-start.4 = (bf16[512,512]{1,0:T(8,128)(2,1)S(1)}, bf16[512,512]{1,0:T(8,128)(2,1)S(1)}, u32[]{:S(2)}, u32[]{:S(2)}) collective-permute-start(bf16[512,512]{1,0:T(8,128)(2,1)S(1)} %constant_dynamic-slice_fusion), channel_id=1, source_target_pairs={{0,1},{1,0},{2,3},{3,2},{4,5},{5,4},{6,7},{7,6},{8,9},{9,8},{10,11... | collective-permute-start | bytes 1572872 | tf_op jit(solution)/shard_map/ppermute | solution.py:628
  36.2 14.4 %collective-permute-start = (bf16[320,768]{1,0:T(8,128)(2,1)}, bf16[320,768]{1,0:T(8,128)(2,1)S(1)}, u32[]{:S(2)}, u32[]{:S(2)}) collective-permute-start(bf16[320,768]{1,0:T(8,128)(2,1)} %get-tuple-element.180.in2_ref.refs_0_), channel_id=1, source_target_pairs={{0,1},{1,0},{2,3},{3,2},{4,5},{5,4},{6,7},{7,6},{8,9},{9,8},{10,11... | collective-permute-start | bytes 1474568 | tf_op jit(solution)/shard_map/ppermute | solution.py:807
  36.3 25.6 %collective-permute-start.2 = (bf16[256,1024]{1,0:T(8,128)(2,1)S(1)}, bf16[256,1024]{1,0:T(8,128)(2,1)}, u32[]{:S(2)}, u32[]{:S(2)}) collective-permute-start(bf16[256,1024]{1,0:T(8,128)(2,1)S(1)} %constant_dynamic-slice_fusion.1), channel_id=1, source_target_pairs={{0,1},{1,0},{2,3},{3,2},{4,5},{5,4},{6,7},{7,6},{8,9},{9,8},{10,11... | collective-permute-start | bytes 1572872 | tf_op jit(solution)/shard_map/ppermute | solution.py:628
  38.4 38.3 %collective-permute-start.5 = (bf16[512,512]{1,0:T(8,128)(2,1)S(1)}, bf16[512,512]{1,0:T(8,128)(2,1)S(1)}, u32[]{:S(2)}, u32[]{:S(2)}) collective-permute-start(bf16[512,512]{1,0:T(8,128)(2,1)S(1)} %collective-permute-done.4), channel_id=1, source_target_pairs={{0,2},{2,0},{4,6},{6,4},{8,10},{10,8},{12,14},{14,12},{16,18},{18,... | collective-permute-start | bytes 1572872 | tf_op jit(solution)/shard_map/ppermute | solution.py:641
  56.7 14.2 %collective-permute-start.1 = (bf16[320,768]{1,0:T(8,128)(2,1)}, bf16[320,768]{1,0:T(8,128)(2,1)S(1)}, u32[]{:S(2)}, u32[]{:S(2)}) collective-permute-start(bf16[320,768]{1,0:T(8,128)(2,1)} %get-tuple-element.183._), channel_id=1, source_target_pairs={{0,1},{1,0},{2,3},{3,2},{4,5},{5,4},{6,7},{7,6},{8,9},{9,8},{10,11... | collective-permute-start | bytes 1474568 | tf_op jit(solution)/shard_map/ppermute | solution.py:815
  61.9 18.1 %collective-permute-start.3 = (bf16[256,1024]{1,0:T(8,128)(2,1)}, bf16[256,1024]{1,0:T(8,128)(2,1)S(1)}, u32[]{:S(2)}, u32[]{:S(2)}) collective-permute-start(bf16[256,1024]{1,0:T(8,128)(2,1)} %collective-permute-done.2), channel_id=1, source_target_pairs={{0,2},{2,0},{4,6},{6,4},{8,10},{10,8},{12,14},{14,12},{16,18},{18,... | collective-permute-start | bytes 1572872 | tf_op jit(solution)/shard_map/ppermute | solution.py:641
  209.5 36.4 %collective-permute-start.11 = (bf16[2,8,48,768]{3,2,1,0:T(8,128)(2,1)}, bf16[2,8,48,768]{3,2,1,0:T(8,128)(2,1)S(1)}, u32[]{:S(2)}, u32[]{:S(2)}) collective-permute-start(bf16[2,8,48,768]{3,2,1,0:T(8,128)(2,1)} %get-tuple-element.220), channel_id=1, source_target_pairs={{0,2},{2,0},{4,6},{6,4},{8,10},{10,8},{12,14},{14,12},{16,18},{18,... | collective-permute-start | bytes 3538952 | tf_op jit(solution)/shard_map/ppermute | solution.py:641
  209.5 38.9 %collective-permute-start.8 = (bf16[2,8,24,1536]{3,2,1,0:T(8,128)(2,1)}, bf16[2,8,24,1536]{3,2,1,0:T(8,128)(2,1)S(1)}, u32[]{:S(2)}, u32[]{:S(2)}) collective-permute-start(bf16[2,8,24,1536]{3,2,1,0:T(8,128)(2,1)} %get-tuple-element.218), channel_id=1, source_target_pairs={{0,2},{2,0},{4,6},{6,4},{8,10},{10,8},{12,14},{14,12},{16,18},{18,... | collective-permute-start | bytes 3538952 | tf_op jit(solution)/shard_map/ppermute | solution.py:641
  210.1 13.1 %collective-permute-start.7 = (bf16[320,768]{1,0:T(8,128)(2,1)S(1)}, bf16[320,768]{1,0:T(8,128)(2,1)S(1)}, u32[]{:S(2)}, u32[]{:S(2)}) collective-permute-start(bf16[320,768]{1,0:T(8,128)(2,1)S(1)} %copy-done.98), channel_id=1, source_target_pairs={{0,1},{1,0},{2,3},{3,2},{4,5},{5,4},{6,7},{7,6},{8,9},{9,8},{10,11... | collective-permute-start | bytes 1474568 | tf_op jit(solution)/shard_map/ppermute | solution.py:852
  212.4 129.8 %reduce-scatter.3.cloned.1.call-start = ((), (), s32[]{:S(2)}) async-start(), calls=%async_computation.2 | async-start | bytes 2228224 | tf_op jit(solution)/shard_map/reduce_scatter | solution.py:651
  245.9 32.8 %collective-permute-start.22 = (bf16[2,8,2,472,128]{4,3,2,1,0:T(8,128)(2,1)}, bf16[2,8,2,472,128]{4,3,2,1,0:T(8,128)(2,1)}, u32[]{:S(2)}, u32[]{:S(2)}) collective-permute-start(bf16[2,8,2,472,128]{4,3,2,1,0:T(8,128)(2,1)} %get-tuple-element.230), channel_id=1, source_target_pairs={{0,2},{2,0},{4,6},{6,4},{8,10},{10,8},{12,14},{14,12},{16,18},{18,... | collective-permute-start | bytes 11599880 | tf_op jit(solution)/shard_map/ppermute | solution.py:641
  285.3 59.4 %collective-permute-start.24 = (bf16[2,472,128]{2,1,0:T(8,128)(2,1)}, bf16[2,472,128]{2,1,0:T(8,128)(2,1)S(1)}, u32[]{:S(2)}, u32[]{:S(2)}) collective-permute-start(bf16[2,472,128]{2,1,0:T(8,128)(2,1)} %dynamic-slice_bitcast_fusion), channel_id=1, source_target_pairs={{0,4},{2,6},{8,0},{10,2},{16,8},{18,10},{24,16},{26,18},{28,24},{3... | collective-permute-start | bytes 725000 | tf_op jit(solution)/shard_map/ppermute | solution.py:669
  287.5 60.3 %collective-permute-start.73 = (bf16[2,32,512]{2,1,0:T(8,128)(2,1)}, bf16[2,32,512]{2,1,0:T(8,128)(2,1)S(1)}, u32[]{:S(2)}, u32[]{:S(2)}) collective-permute-start(bf16[2,32,512]{2,1,0:T(8,128)(2,1)} %dynamic-slice_bitcast_fusion.6), channel_id=1, source_target_pairs={{0,1},{1,0},{2,3},{3,2},{4,5},{5,4},{6,7},{7,6},{8,9},{9,8},{10,11... | collective-permute-start | bytes 196616 | tf_op jit(solution)/shard_map/ppermute | solution.py:680
  289.7 55.9 %collective-permute-start.23 = (bf16[2,472,128]{2,1,0:T(8,128)(2,1)}, bf16[2,472,128]{2,1,0:T(8,128)(2,1)}, u32[]{:S(2)}, u32[]{:S(2)}) collective-permute-start(bf16[2,472,128]{2,1,0:T(8,128)(2,1)} %dynamic-slice_bitcast_fusion.1), channel_id=1, source_target_pairs={{0,8},{2,10},{8,16},{10,18},{16,24},{18,26},{24,28},{26,30},{28,20... | collective-permute-start | bytes 725000 | tf_op jit(solution)/shard_map/ppermute | solution.py:669
  343.2 20.4 %collective-permute-start.72 = (bf16[2,16,1024]{2,1,0:T(8,128)(2,1)S(1)}, bf16[2,16,1024]{2,1,0:T(8,128)(2,1)S(1)}, u32[]{:S(2)}, u32[]{:S(2)}) collective-permute-start(bf16[2,16,1024]{2,1,0:T(8,128)(2,1)S(1)} %dynamic-slice_bitcast_fusion.7), channel_id=1, source_target_pairs={{0,1},{1,0},{2,3},{3,2},{4,5},{5,4},{6,7},{7,6},{8,9},{9,8},{10,11... | collective-permute-start | bytes 196616 | tf_op jit(solution)/shard_map/ppermute | solution.py:680
  347.8 14.7 %collective-permute-start.30 = (bf16[2,472,128]{2,1,0:T(8,128)(2,1)S(1)}, bf16[2,472,128]{2,1,0:T(8,128)(2,1)S(1)}, u32[]{:S(2)}, u32[]{:S(2)}) collective-permute-start(bf16[2,472,128]{2,1,0:T(8,128)(2,1)S(1)} %bitcast_add_fusion.12), channel_id=1, source_target_pairs={{0,4},{2,6},{8,0},{10,2},{16,8},{18,10},{24,16},{26,18},{28,24},{3... | collective-permute-start | bytes 725000 | tf_op jit(solution)/shard_map/ppermute | solution.py:669
  349.5 13.1 %collective-permute-start.29 = (bf16[2,472,128]{2,1,0:T(8,128)(2,1)S(1)}, bf16[2,472,128]{2,1,0:T(8,128)(2,1)S(1)}, u32[]{:S(2)}, u32[]{:S(2)}) collective-permute-start(bf16[2,472,128]{2,1,0:T(8,128)(2,1)S(1)} %bitcast_add_fusion.13), channel_id=1, source_target_pairs={{0,8},{2,10},{8,16},{10,18},{16,24},{18,26},{24,28},{26,30},{28,20... | collective-permute-start | bytes 725000 | tf_op jit(solution)/shard_map/ppermute | solution.py:669
  390.4 12.4 %collective-permute-start.48 = (bf16[2,472,128]{2,1,0:T(8,128)(2,1)S(1)}, bf16[2,472,128]{2,1,0:T(8,128)(2,1)S(1)}, u32[]{:S(2)}, u32[]{:S(2)}) collective-permute-start(bf16[2,472,128]{2,1,0:T(8,128)(2,1)S(1)} %bitcast_add_fusion.6), channel_id=1, source_target_pairs={{0,4},{2,6},{8,0},{10,2},{16,8},{18,10},{24,16},{26,18},{28,24},{3... | collective-permute-start | bytes 725000 | tf_op jit(solution)/shard_map/ppermute | solution.py:669
  390.4 12.4 %collective-permute-start.47 = (bf16[2,472,128]{2,1,0:T(8,128)(2,1)S(1)}, bf16[2,472,128]{2,1,0:T(8,128)(2,1)S(1)}, u32[]{:S(2)}, u32[]{:S(2)}) collective-permute-start(bf16[2,472,128]{2,1,0:T(8,128)(2,1)S(1)} %bitcast_add_fusion.7), channel_id=1, source_target_pairs={{0,8},{2,10},{8,16},{10,18},{16,24},{18,26},{24,28},{26,30},{28,20... | collective-permute-start | bytes 725000 | tf_op jit(solution)/shard_map/ppermute | solution.py:669
  463.8 21.0 %collective-permute-start.84 = (bf16[24,1536]{1,0:T(8,128)(2,1)S(1)}, bf16[24,1536]{1,0:T(8,128)(2,1)S(1)}, u32[]{:S(2)}, u32[]{:S(2)}) collective-permute-start(bf16[24,1536]{1,0:T(8,128)(2,1)S(1)} %collective-permute-done.74.refs_5_), channel_id=1, source_target_pairs={{0,8},{2,10},{8,16},{10,18},{16,24},{18,26},{24,28},{26,30},{28,20... | collective-permute-start | bytes 221192 | tf_op jit(solution)/shard_map/ppermute | solution.py:688
  465.2 15.5 %collective-permute-start.90 = (bf16[16,1024]{1,0:T(8,128)(2,1)}, bf16[16,1024]{1,0:T(8,128)(2,1)S(1)}, u32[]{:S(2)}, u32[]{:S(2)}) collective-permute-start(bf16[16,1024]{1,0:T(8,128)(2,1)} %collective-permute-done.80.refs_1_), channel_id=1, source_target_pairs={{0,8},{2,10},{8,16},{10,18},{16,24},{18,26},{24,28},{26,30},{28,20... | collective-permute-start | bytes 98312 | tf_op jit(solution)/shard_map/ppermute | solution.py:688
  465.8 15.4 %collective-permute-start.91 = (bf16[16,1024]{1,0:T(8,128)(2,1)}, bf16[16,1024]{1,0:T(8,128)(2,1)S(1)}, u32[]{:S(2)}, u32[]{:S(2)}) collective-permute-start(bf16[16,1024]{1,0:T(8,128)(2,1)} %collective-permute-done.81.refs_9_), channel_id=1, source_target_pairs={{0,4},{2,6},{8,0},{10,2},{16,8},{18,10},{24,16},{26,18},{28,24},{3... | collective-permute-start | bytes 98312 | tf_op jit(solution)/shard_map/ppermute | solution.py:688
  467.5 15.3 %collective-permute-start.92 = (bf16[32,512]{1,0:T(8,128)(2,1)}, bf16[32,512]{1,0:T(8,128)(2,1)S(1)}, u32[]{:S(2)}, u32[]{:S(2)}) collective-permute-start(bf16[32,512]{1,0:T(8,128)(2,1)} %collective-permute-done.82.refs_1_), channel_id=1, source_target_pairs={{0,8},{2,10},{8,16},{10,18},{16,24},{18,26},{24,28},{26,30},{28,20... | collective-permute-start | bytes 98312 | tf_op jit(solution)/shard_map/ppermute | solution.py:688
  467.9 15.4 %collective-permute-start.93 = (bf16[32,512]{1,0:T(8,128)(2,1)}, bf16[32,512]{1,0:T(8,128)(2,1)S(1)}, u32[]{:S(2)}, u32[]{:S(2)}) collective-permute-start(bf16[32,512]{1,0:T(8,128)(2,1)} %collective-permute-done.83.refs_9_), channel_id=1, source_target_pairs={{0,4},{2,6},{8,0},{10,2},{16,8},{18,10},{24,16},{26,18},{28,24},{3... | collective-permute-start | bytes 98312 | tf_op jit(solution)/shard_map/ppermute | solution.py:688
  514.6 13.9 %collective-permute-start.110 = (bf16[472,128]{1,0:T(8,128)(2,1)S(1)}, bf16[472,128]{1,0:T(8,128)(2,1)S(1)}, u32[]{:S(2)}, u32[]{:S(2)}) collective-permute-start(bf16[472,128]{1,0:T(8,128)(2,1)S(1)} %collective-permute-done.104.refs_5_), channel_id=1, source_target_pairs={{0,8},{2,10},{8,16},{10,18},{16,24},{18,26},{24,28},{26,30},{28,20... | collective-permute-start | bytes 362504 | tf_op jit(solution)/shard_map/ppermute | solution.py:688
  515.9 12.7 %collective-permute-start.111 = (bf16[472,128]{1,0:T(8,128)(2,1)S(1)}, bf16[472,128]{1,0:T(8,128)(2,1)S(1)}, u32[]{:S(2)}, u32[]{:S(2)}) collective-permute-start(bf16[472,128]{1,0:T(8,128)(2,1)S(1)} %collective-permute-done.105.refs_13_), channel_id=1, source_target_pairs={{0,4},{2,6},{8,0},{10,2},{16,8},{18,10},{24,16},{26,18},{28,24},{3... | collective-permute-start | bytes 362504 | tf_op jit(solution)/shard_map/ppermute | solution.py:688
  528.6 12.1 %collective-permute-start.116 = (bf16[472,128]{1,0:T(8,128)(2,1)S(1)}, bf16[472,128]{1,0:T(8,128)(2,1)S(1)}, u32[]{:S(2)}, u32[]{:S(2)}) collective-permute-start(bf16[472,128]{1,0:T(8,128)(2,1)S(1)} %collective-permute-done.110.refs_6_), channel_id=1, source_target_pairs={{0,8},{2,10},{8,16},{10,18},{16,24},{18,26},{24,28},{26,30},{28,20... | collective-permute-start | bytes 362504 | tf_op jit(solution)/shard_map/ppermute | solution.py:688
  540.6 29.8 %collective-permute-start.122 = (bf16[12,472,128]{2,1,0:T(8,128)(2,1)}, bf16[12,472,128]{2,1,0:T(8,128)(2,1)S(1)}, u32[]{:S(2)}, u32[]{:S(2)}) collective-permute-start(bf16[12,472,128]{2,1,0:T(8,128)(2,1)} %constant_dynamic-update-slice_fusion), channel_id=1, source_target_pairs={{0,2},{2,0},{4,6},{6,4},{8,10},{10,8},{12,14},{14,12},{16,18},{18,... | collective-permute-start | bytes 4349960 | tf_op jit(solution)/shard_map/ppermute | solution.py:641
  544.8 14.6 %collective-permute-start.126 = (bf16[12,48,768]{2,1,0:T(8,128)(2,1)}, bf16[12,48,768]{2,1,0:T(8,128)(2,1)S(1)}, u32[]{:S(2)}, u32[]{:S(2)}) collective-permute-start(bf16[12,48,768]{2,1,0:T(8,128)(2,1)} %constant_dynamic-update-slice_fusion.24), channel_id=1, source_target_pairs={{0,2},{2,0},{4,6},{6,4},{8,10},{10,8},{12,14},{14,12},{16,18},{18,... | collective-permute-start | bytes 2654216 | tf_op jit(solution)/shard_map/ppermute | solution.py:641
  548.1 16.5 %collective-permute-start.124 = (bf16[12,24,1536]{2,1,0:T(8,128)(2,1)}, bf16[12,24,1536]{2,1,0:T(8,128)(2,1)S(1)}, u32[]{:S(2)}, u32[]{:S(2)}) collective-permute-start(bf16[12,24,1536]{2,1,0:T(8,128)(2,1)} %constant_dynamic-update-slice_fusion.12), channel_id=1, source_target_pairs={{0,2},{2,0},{4,6},{6,4},{8,10},{10,8},{12,14},{14,12},{16,18},{18,... | collective-permute-start | bytes 2654216 | tf_op jit(solution)/shard_map/ppermute | solution.py:641
  551.4 19.0 %collective-permute-start.123 = (bf16[4,472,128]{2,1,0:T(8,128)(2,1)S(1)}, bf16[4,472,128]{2,1,0:T(8,128)(2,1)S(1)}, u32[]{:S(2)}, u32[]{:S(2)}) collective-permute-start(bf16[4,472,128]{2,1,0:T(8,128)(2,1)S(1)} %pad_maximum_fusion.2), channel_id=1, source_target_pairs={{0,2},{2,0},{4,6},{6,4},{8,10},{10,8},{12,14},{14,12},{16,18},{18,... | collective-permute-start | bytes 1449992 | tf_op jit(solution)/shard_map/ppermute | solution.py:641
  (205 other events, 4253.5 us)
Sparse Core Ops, SparseCore 0:
  212.5 64.2 reduce-scatter.4
  281.6 60.5 reduce-scatter.2
